TPU v7x, 32 devices: a whole 2x2x4 slice. The times are simulated.
32 devices in a mesh: fsdp: 16 (over z, x, core), tp: 2 (over y).
Axes of the slice: x: 2, y: 2, z: 4, core: 2. Of those that a mesh axis runs over, the one named last changes fastest.
Arguments:
- hidden: bfloat16 [16384, 768], P(('fsdp', 'tp')), may hold values from -6 to 6
- prev_logits: float32 [16384, 12], P(('fsdp', 'tp')), may hold values from -4 to 4
- routes: int32 [16384, 2], P(('fsdp', 'tp')), may hold values from 0 to 11, as said below
- slot_rank: int32 [16384, 2], P(('fsdp', 'tp')), may hold values from 0 to 191, as said below
- dropped: int32 [16384, 2], P(('fsdp', 'tp')), may hold values from 0 to 1, as said below
- cotangent: bfloat16 [16384, 768], P(('fsdp', 'tp')), may hold values from -6 to 6
- attn_norm: bfloat16 [768], P(('fsdp', 'tp')), may hold values from 0.5 to 1.5
- ffn_norm: bfloat16 [768], P(('fsdp', 'tp')), may hold values from 0.5 to 1.5
- w_qkv: bfloat16 [768, 3, 768], P('fsdp', None, 'tp'), may hold values from -0.21875 to 0.21875
- w_attn_out: bfloat16 [768, 768], P('fsdp', 'tp'), may hold values from -0.875 to 0.875
- w_router: bfloat16 [768, 12], P(('fsdp', 'tp')), may hold values from -0.109375 to 0.109375
- w_const_gate: bfloat16 [768, 4], P(('fsdp', 'tp')), may hold values from -0.21875 to 0.21875
- w_const_value: bfloat16 [768, 2], P(('fsdp', 'tp')), may hold values from -5 to 5
- w_expert_in: bfloat16 [8, 768, 2, 2048], P(None, 'fsdp', None, 'tp'), may hold values from -0.21875 to 0.21875
- w_expert_out: bfloat16 [8, 768, 2048], P(None, 'fsdp', 'tp'), may hold values from -0.25 to 0.25
Outputs:
- output: bfloat16 [16384, 768], P(('fsdp', 'tp'))
- grad_hidden: float32 [16384, 768], P(('fsdp', 'tp'))
- grad_attn_norm: float32 [768], P(('fsdp', 'tp'))
- grad_ffn_norm: float32 [768], P(('fsdp', 'tp'))
- grad_qkv: float32 [768, 3, 768], P('fsdp', None, 'tp')
- grad_attn_out: float32 [768, 768], P('fsdp', 'tp')
- grad_router: float32 [768, 12], P(('fsdp', 'tp'))
- grad_const_gate: float32 [768, 4], P(('fsdp', 'tp'))
- grad_const_value: float32 [768, 2], P(('fsdp', 'tp'))
- grad_expert_in: float32 [8, 768, 2, 2048], P(None, 'fsdp', None, 'tp')
- grad_expert_out: float32 [8, 768, 2048], P(None, 'fsdp', 'tp')
Inputs may be any that keep to these rules, and one draw needn't show every extreme that they name: `routes`: each token names two different experts; experts 0 to 7 are feed-forward, 8 the zero expert, 9 the copy expert, 10 and 11 the constant ones. `slot_rank`: for a kept pair to a feed-forward expert: the number of earlier pairs of its sequence kept by the same expert (tokens in order, a token's first expert before its second), so that kept pairs of one expert fill slots 0 upward without gaps; 0 for all other pairs. `dropped`: 1 exactly for pairs to a feed-forward expert that come after 192 earlier pairs of their sequence to that expert.
All inputs are finite; a program needn't handle non-finite values.
Results may differ from a plain program's by a relative error of at most 0.018.
Values may be sent and summed in bfloat16 or wider, within the bound.
A program may use at most 256 MiB of HBM per device.

v0:
```python
import functools

import jax
import jax.numpy as jnp
import numpy as np
from jax import lax
from jax.experimental import pallas as pl
from jax.experimental.pallas import tpu as pltpu
from jax.sharding import PartitionSpec as P

HD = 64
BLOCK = 256


EPSILON = 1e-06
MESH = pl.DeviceIdType.MESH
PAIR = 2 * HD
SCALING = HD ** (-0.5)
ROUTER = 2
MIXING = 14
VALUE = 18
ROUTE = 20
TARGET = 24
GATE = 26
COPY = 9


TILE = 256


def swap(values):
    return lax.ppermute(values, "tp", [(0, 1), (1, 0)])


def gather_rows(values):
    other = swap(values)
    first = lax.axis_index("tp") == 0
    return jnp.concatenate(
        [jnp.where(first, values, other), jnp.where(first, other, values)], axis=0
    )


def own_half(values):
    half = values.shape[0] // 2
    return lax.dynamic_slice_in_dim(values, lax.axis_index("tp") * half, half, 0)


def other_half(values):
    half = values.shape[0] // 2
    return lax.dynamic_slice_in_dim(values, (1 - lax.axis_index("tp")) * half, half, 0)


def member_groups(size, experts):
    span = 2 * experts
    starts = range(0, size, span)
    cores = [[start + 2 * e, start + 2 * e + 1] for start in starts for e in range(experts)]
    across = [[start + r for start in starts] for r in range(span)]
    return cores, across


def own_core(values, rows):
    parts = values.reshape(-1, 2, rows, values.shape[-1])
    return lax.dynamic_index_in_dim(parts, lax.axis_index("fsdp") % 2, 1, keepdims=False)


def join_weights(got, experts):
    size = lax.axis_size("fsdp")
    if size == 2 * experts:
        return got
    cores, across = member_groups(size, experts)
    got = lax.all_gather(got, "fsdp", axis=1, axis_index_groups=cores, tiled=True)
    got = got.reshape(-1, got.shape[-1])
    got = lax.all_gather(got, "fsdp", axis=0, axis_index_groups=across, tiled=True)
    return own_core(got, got.shape[0] // (2 * experts))


def split_grads(grads):
    experts, _, columns = grads.shape
    size = lax.axis_size("fsdp")
    if size == 2 * experts:
        return grads
    cores, across = member_groups(size, experts)
    grads = lax.all_gather(grads[:, None], "fsdp", axis=1, axis_index_groups=cores, tiled=True)
    grads = grads.reshape(-1, columns)
    grads = lax.psum_scatter(
        grads, "fsdp", scatter_dimension=0, axis_index_groups=across, tiled=True
    )
    return own_core(grads, grads.shape[0] // (2 * experts))


def finish_plain(big, wqkv, other):
    heads_width = (big.shape[1] - PAIR) // 4
    reduced = wide(lax.psum_scatter(big, "fsdp", scatter_dimension=0, tiled=True))
    parts = reduced[:, : 3 * heads_width].reshape(-1, 3, heads_width).transpose(1, 0, 2)
    share = jnp.sum(parts * wide(wqkv), axis=(0, 2))
    last = jnp.concatenate([share[:, None], reduced[:, 4 * heads_width + 1 :]], axis=1)
    return (
        swap(other),
        reduced[:, : 4 * heads_width],
        own_half(last) + swap(other_half(last)),
    )


def forward_plain(operands, table):
    (
        hidden,
        cotangent,
        logits,
        routes,
        rank,
        dropped,
        gains,
        router,
        mixing,
        value,
        wqkv,
        wout,
        w_in,
        w_down,
    ) = operands
    own_rows, width = hidden.shape
    experts, shard, units = w_down.shape
    small = jnp.concatenate([wide(v) for v in (gains, router, mixing, value)], axis=0)
    small = jnp.pad(small, ((0, PAIR - small.shape[0]), (0, 0))).T
    small = lax.all_gather(small, ("fsdp", "tp"), axis=0, tiled=True)
    capacity = own_rows * 2 * 9 // 48
    kept = (routes < experts) & (dropped == 0)
    target = jnp.where(kept, routes * capacity + rank, -1)
    blank = jnp.zeros((2, own_rows), jnp.float32)
    tok = jnp.concatenate(
        [blank, logits, blank, blank, blank, wide(routes), blank, wide(target)], axis=0
    )
    tok = lax.all_gather(tok, "tp", axis=1, tiled=True).T
    tok = jnp.pad(tok, ((0, 0), (0, PAIR - tok.shape[1])))
    blocks = jnp.concatenate([wqkv[0], wqkv[1], wqkv[2], wout], axis=1)
    blocks = lax.all_gather(blocks, "fsdp", axis=0, tiled=True).reshape(2 * experts, -1, blocks.shape[1])
    rows = small.T[:8]
    small = low(small)
    shards_flat = jnp.concatenate([w_in.reshape(experts, shard, 2 * units), w_down], axis=2)
    return (blocks, small, rows) + tuple(
        run_forward_plain(
            gather_rows(hidden), tok, blocks, small, rows, table, shards_flat, cotangent
        )
    )


def nt_dot(left, right):
    return lax.dot_general(left, right, (((1,), (1,)), ((), ())), preferred_element_type=jnp.float32)


def nn_dot(left, right):
    return jnp.dot(left, right, preferred_element_type=jnp.float32)


def tn_dot(left, right):
    return lax.dot_general(left, right, (((0,), (0,)), ((), ())), preferred_element_type=jnp.float32)


def low(values):
    return values.astype(jnp.bfloat16)


def wide(values):
    return values.astype(jnp.float32)


def rotary_table(length):
    half = HD // 2
    positions = np.arange(length, dtype=np.float32)
    inverse = np.power(np.float32(10000.0), -np.arange(half, dtype=np.float32) / np.float32(half))
    angles = (positions[:, None] * inverse[None, :].astype(np.float32)).astype(np.float32)
    cosine = np.cos(angles.astype(np.float64)).astype(np.float32)
    sine = np.sin(angles.astype(np.float64)).astype(np.float32)
    both = np.concatenate([cosine, sine], axis=1)
    return np.concatenate([both[: length // 2], both[length // 2 :]], axis=1)


def spread_table(table_ref, block):
    quarter = HD // 2
    blocks = table_ref.shape[0] // BLOCK
    table = table_ref[block_rows(lax.rem(block, blocks)), :]
    table = jnp.where(block >= blocks, pltpu.roll(table, HD, 1), table)
    lane = lax.broadcasted_iota(jnp.int32, table.shape, 1)
    cosine = jnp.where(lane < quarter, table, 0.0)
    cosine = cosine + pltpu.roll(cosine, quarter, 1)
    sine = jnp.where(jnp.logical_and(lane >= quarter, lane < HD), table, 0.0)
    sine = sine - pltpu.roll(sine, PAIR - quarter, 1)
    return cosine + pltpu.roll(cosine, HD, 1), sine + pltpu.roll(sine, HD, 1)


def turn(values, cosine, sine):
    lane = lax.broadcasted_iota(jnp.int32, values.shape, 1)
    upper = lax.rem(lane, HD) >= HD // 2
    partner = jnp.where(
        upper, pltpu.roll(values, HD // 2, 1), pltpu.roll(values, PAIR - HD // 2, 1)
    )
    return values * cosine + partner * sine


def head_lanes(shape, half, axis):
    return (lax.broadcasted_iota(jnp.int32, shape, axis) >= HD) == bool(half)


def mean_last(values):
    return jnp.mean(values, axis=-1, keepdims=True)


def to_partner(source, target, send_sem, recv_sem):
    return pltpu.make_async_remote_copy(
        src_ref=source,
        dst_ref=target,
        send_sem=send_sem,
        recv_sem=recv_sem,
        device_id={"tp": 1 - lax.axis_index("tp")},
        device_id_type=MESH,
    )


def block_rows(block):
    return pl.ds(pl.multiple_of(block * BLOCK, BLOCK), BLOCK)


def column(values, index):
    return values[:, index : index + 1]


def lane_matrix(shape, columns):
    lane = lax.broadcasted_iota(jnp.int32, shape, 1)
    total = jnp.zeros(shape, jnp.float32)
    for index, values in columns:
        total = jnp.where(lane == index, values, total)
    return total


def send_to(source, target, send_sem, recv_sem, device):
    return pltpu.make_async_remote_copy(
        src_ref=source,
        dst_ref=target,
        send_sem=send_sem,
        recv_sem=recv_sem,
        device_id=device,
        device_id_type=MESH,
    )


def greet_group(peers):
    me = lax.axis_index("fsdp")
    rank = lax.rem(me, peers)
    barrier = pltpu.get_barrier_semaphore()
    for k in range(1, peers):
        pl.semaphore_signal(
            barrier,
            inc=1,
            device_id={"fsdp": me - rank + lax.rem(rank + k, peers)},
            device_id_type=MESH,
        )
    pl.semaphore_signal(
        barrier, inc=1, device_id={"tp": 1 - lax.axis_index("tp")}, device_id_type=MESH
    )
    pl.semaphore_wait(barrier, peers)


def each(first, last, body):
    def step(k, carry):
        body(k)
        return carry

    lax.fori_loop(first, last, step, 0)


def flipped(value, k, bits):
    other = 0
    bit = 1
    while bit < bits:
        ours, theirs = lax.rem(value // bit, 2), lax.rem(k // bit, 2)
        other = other + bit * (ours + theirs - 2 * ours * theirs)
        bit *= 2
    return other


class CoreExchange:
    def __init__(self, source, target, send_sem, recv_sem):
        experts = source.shape[0]
        me = lax.axis_index("fsdp")
        rank = lax.rem(me, 2 * experts)
        core = lax.rem(rank, 2)
        mine = rank // 2

        def device(k):
            return {"fsdp": me - rank + 2 * flipped(mine, k, experts) + core}

        def copy(k):
            there = flipped(mine, k, experts)
            return send_to(
                source.at[there], target.at[mine], send_sem.at[k], recv_sem.at[k], device(k)
            )

        def arrival(k):
            there = flipped(mine, k, experts)
            return send_to(
                source.at[there], target.at[there], send_sem.at[k], recv_sem.at[k], device(k)
            )

        self.experts, self.copy, self.arrival = experts, copy, arrival
        self.local = pltpu.make_async_copy(source.at[mine], target.at[mine], send_sem.at[0])

    def start(self):
        self.local.start()
        each(1, self.experts, lambda k: self.copy(k).start())

    def wait(self):
        each(1, self.experts, lambda k: self.copy(k).wait_send())
        each(1, self.experts, lambda k: self.arrival(k).wait_recv())
        self.local.wait()


def finish_kernel(
    big_ref,
    wqkv_ref,
    other_ref,
    y_ref,
    red_ref,
    tail_ref,
    sum_ref,
    core_ref,
    side_ref,
    acc_ref,
    usend_ref,
    urecv_ref,
    dsend_ref,
    drecv_ref,
    tsend_ref,
    trecv_ref,
    core_send,
    core_recv,
    x_send,
    x_recv,
    up_send,
    up_recv,
    dn_send,
    dn_recv,
    y_send,
    y_recv,
):
    size = big_ref.shape[0]
    planes = size // 4
    me = lax.axis_index("fsdp")
    tp = lax.axis_index("tp")
    z, x, core = me // 4, lax.rem(me // 2, 2), lax.rem(me, 2)
    heads_width = wqkv_ref.shape[2]
    greet_group(size)
    partner = {"tp": 1 - tp}

    def to_core(plane, line):
        slot = plane * 2 + line
        return send_to(
            big_ref.at[plane * 4 + line * 2 + 1 - core],
            core_ref.at[slot],
            core_send.at[slot],
            core_recv.at[slot],
            {"fsdp": me + 1 - 2 * core},
        )

    def to_side(plane):
        return send_to(
            sum_ref.at[plane],
            side_ref.at[plane],
            x_send.at[plane],
            x_recv.at[plane],
            {"fsdp": z * 4 + (1 - x) * 2 + core},
        )

    def to_up(plane):
        return send_to(
            usend_ref.at[plane],
            urecv_ref.at[plane],
            up_send.at[plane],
            up_recv.at[plane],
            {"fsdp": lax.min(z + 1, planes - 1) * 4 + x * 2 + core},
        )

    def to_down(plane):
        return send_to(
            dsend_ref.at[plane],
            drecv_ref.at[plane],
            dn_send.at[plane],
            dn_recv.at[plane],
            {"fsdp": lax.max(z - 1, 0) * 4 + x * 2 + core},
        )

    lower = z < planes // 2
    order = [jnp.where(lower, planes - 1 - step, step) for step in range(planes)]
    for plane in order:
        to_core(plane, 1 - x).start()
    for plane in order:
        to_core(plane, x).start()
    out_y = send_to(other_ref, y_ref, y_send.at[0], y_recv.at[0], partner)
    out_y.start()

    def joined(plane, line):
        to_core(plane, line).wait_recv()
        return wide(big_ref[plane * 4 + line * 2 + core]) + wide(core_ref[plane * 2 + line])

    for plane in order:
        sum_ref[plane] = low(joined(plane, 1 - x))
        to_side(plane).start()
    for plane in order:
        acc_ref[plane] = joined(plane, x)

    def rise(plane):
        @pl.when(z < plane)
        def _():
            @pl.when(z > 0)
            def _():
                to_up(plane).wait_recv()
                acc_ref[plane] += wide(urecv_ref[plane])

            usend_ref[plane] = low(acc_ref[plane])
            to_up(plane).start()

    def fall(plane):
        @pl.when(z > plane)
        def _():
            @pl.when(z < planes - 1)
            def _():
                to_down(plane).wait_recv()
                acc_ref[plane] += wide(drecv_ref[plane])

            dsend_ref[plane] = low(acc_ref[plane])
            to_down(plane).start()

    for step, plane in enumerate(order):
        to_side(plane).wait_recv()
        acc_ref[plane] += wide(side_ref[plane])
        last_step = step == planes - 1

        @pl.when(lower)
        def _():
            (fall if last_step else rise)(plane)

        @pl.when(jnp.logical_not(lower))
        def _():
            (rise if last_step else fall)(plane)

    @pl.when(z > 0)
    def _():
        to_up(z).wait_recv()
        acc_ref[z] += wide(urecv_ref[z])

    @pl.when(z < planes - 1)
    def _():
        to_down(z).wait_recv()
        acc_ref[z] += wide(drecv_ref[z])

    values = acc_ref[z]
    red_ref[...] = values[:, : 4 * heads_width]
    share = sum(
        jnp.sum(
            values[:, part * heads_width : (part + 1) * heads_width] * wide(wqkv_ref[part]),
            axis=1,
            keepdims=True,
        )
        for part in range(3)
    )
    last = values[:, 4 * heads_width :]
    last = jnp.where(lax.broadcasted_iota(jnp.int32, last.shape, 1) == 0, share, last)
    part_rows = tail_ref.shape[0]
    tsend_ref[0] = last[:part_rows, :]
    tsend_ref[1] = last[part_rows:, :]
    tail_y = send_to(tsend_ref.at[1 - tp], trecv_ref, y_send.at[1], y_recv.at[1], partner)
    tail_y.start()
    out_y.wait()
    tail_y.wait()
    tail_ref[...] = tsend_ref[tp] + trecv_ref[...]
    for plane in range(planes):
        to_core(plane, 1 - x).wait_send()
        to_core(plane, x).wait_send()
        to_side(plane).wait_send()

        @pl.when(z < plane)
        def _():
            to_up(plane).wait_send()

        @pl.when(z > plane)
        def _():
            to_down(plane).wait_send()


def run_finish(big, wqkv, other):
    size = lax.axis_size("fsdp")
    planes = size // 4
    own_rows, width = other.shape
    columns = big.shape[1]
    shard = width // size
    vmem = pl.BlockSpec(memory_space=pltpu.VMEM)
    low_t, wide_t = jnp.bfloat16, jnp.float32
    dma = pltpu.SemaphoreType.DMA
    line = (planes, shard, columns)
    return pl.pallas_call(
        finish_kernel,
        in_specs=[vmem] * 3,
        out_specs=[vmem] * 3,
        out_shape=[
            jax.ShapeDtypeStruct((own_rows, width), low_t),
            jax.ShapeDtypeStruct((shard, columns - PAIR), wide_t),
            jax.ShapeDtypeStruct((shard // 2, PAIR), wide_t),
        ],
        scratch_shapes=[
            pltpu.VMEM(line, low_t),
            pltpu.VMEM((2 * planes, shard, columns), low_t),
            pltpu.VMEM(line, low_t),
            pltpu.VMEM(line, wide_t),
            pltpu.VMEM(line, low_t),
            pltpu.VMEM(line, low_t),
            pltpu.VMEM(line, low_t),
            pltpu.VMEM(line, low_t),
            pltpu.VMEM((2, shard // 2, PAIR), wide_t),
            pltpu.VMEM((shard // 2, PAIR), wide_t),
            dma((2 * planes,)),
            dma((2 * planes,)),
        ]
        + [dma((planes,))] * 6
        + [dma((2,))] * 2,
        compiler_params=pltpu.CompilerParams(
            collective_id=4, has_side_effects=True, vmem_limit_bytes=60 << 20
        ),
    )(big.reshape(size, shard, columns), wqkv, other)


def write_kernel(
    base_ref,
    y_ref,
    grad_ref,
    red_ref,
    tail_ref,
    gain_ref,
    expert_ref,
    out_ref,
    hidden_ref,
    qkv_ref,
    attn_ref,
    gains_ref,
    router_ref,
    mixing_ref,
    value_ref,
    in_ref,
    down_ref,
):
    hidden = down_ref.shape[2]
    heads_width = attn_ref.shape[1]
    out_ref[...] = low(base_ref[...] + wide(y_ref[...]))
    hidden_ref[...] = grad_ref[...]
    values = wide(expert_ref[0])
    in_ref[0, :, 0, :] = values[:, :hidden]
    in_ref[0, :, 1, :] = values[:, hidden : 2 * hidden]
    down_ref[0] = values[:, 2 * hidden :]

    @pl.when(pl.program_id(0) == 0)
    def _():
        for part in range(3):
            qkv_ref[part] = red_ref[:, part * heads_width : (part + 1) * heads_width]
        attn_ref[...] = red_ref[:, 3 * heads_width :]
        count = tail_ref.shape[0]
        blank = jnp.zeros((PAIR - count, PAIR), jnp.float32)
        turned = jnp.concatenate([tail_ref[...], blank], axis=0).T[:, :count]
        gains_ref[0:1, :] = turned[0:1, :] / gain_ref[0:1, :]
        gains_ref[1:2, :] = turned[1:2, :]
        router_ref[...] = turned[ROUTER:MIXING, :]
        mixing_ref[...] = turned[MIXING:VALUE, :]
        value_ref[...] = turned[VALUE : VALUE + 2, :]


def run_write(base, y, grad_hidden, red, tail, gains, arrived):
    own_rows, width = base.shape
    shard = red.shape[0]
    heads_width = red.shape[1] // 4
    count = tail.shape[0]
    experts, _, total = arrived.shape
    hidden = total // 3
    wide_t = jnp.float32
    rows = pl.BlockSpec((own_rows // experts, width), lambda e: (e, 0))

    def whole(shape):
        return pl.BlockSpec(shape, lambda e: (0,) * len(shape))

    return pl.pallas_call(
        write_kernel,
        grid=(experts,),
        in_specs=[
            rows,
            rows,
            rows,
            whole(red.shape),
            whole(tail.shape),
            whole(gains.shape),
            pl.BlockSpec((1, shard, total), lambda e: (e, 0, 0)),
        ],
        out_specs=[
            rows,
            rows,
            whole((3, shard, heads_width)),
            whole((shard, heads_width)),
            whole((2, count)),
            whole((MIXING - ROUTER, count)),
            whole((VALUE - MIXING, count)),
            whole((2, count)),
            pl.BlockSpec((1, shard, 2, hidden), lambda e: (e, 0, 0, 0)),
            pl.BlockSpec((1, shard, hidden), lambda e: (e, 0, 0)),
        ],
        out_shape=[
            jax.ShapeDtypeStruct((own_rows, width), jnp.bfloat16),
            jax.ShapeDtypeStruct((own_rows, width), wide_t),
            jax.ShapeDtypeStruct((3, shard, heads_width), wide_t),
            jax.ShapeDtypeStruct((shard, heads_width), wide_t),
            jax.ShapeDtypeStruct((2, count), wide_t),
            jax.ShapeDtypeStruct((MIXING - ROUTER, count), wide_t),
            jax.ShapeDtypeStruct((VALUE - MIXING, count), wide_t),
            jax.ShapeDtypeStruct((2, count), wide_t),
            jax.ShapeDtypeStruct((experts, shard, 2, hidden), wide_t),
            jax.ShapeDtypeStruct((experts, shard, hidden), wide_t),
        ],
    )(base, y, grad_hidden, red, tail, gains, arrived)


def expert_kernel(
    s2_ref,
    cot_ref,
    line_ref,
    slot_ref,
    weight_ref,
    res_out_ref,
    dx_out_ref,
    grads_out_ref,
    xs_ref,
    gs_ref,
    x_ref,
    g_ref,
    w_ref,
    gate_ref,
    up_ref,
    act_ref,
    xt_ref,
    gt_ref,
    acc_ref,
    grads_ref,
    sibling_ref,
    ysend_ref,
    yrecv_ref,
    w_sem,
    grad_sem,
    xs_sem,
    xr_sem,
    gs_sem,
    gr_sem,
    xfs_sem,
    xfr_sem,
    gfs_sem,
    gfr_sem,
    ys_sem,
    yr_sem,
    rs_sem,
    rr_sem,
    ds_sem,
    dr_sem,
):
    peers, rows, width = xs_ref.shape
    total = peers * rows
    hidden = gate_ref.shape[1]
    tiles = hidden // TILE
    me = lax.axis_index("fsdp")
    tp = lax.axis_index("tp")
    rank = lax.rem(me, peers)
    core = lax.rem(rank, 2)
    start = me - rank

    def peer(k):
        return {"fsdp": start + flipped(rank, k, peers)}

    partner = {"tp": 1 - tp}
    sibling = {"fsdp": start + rank + 1 - 2 * core}

    def out_x(k):
        return send_to(xs_ref.at[k], x_ref.at[0, k], xs_sem.at[k], xr_sem.at[k], peer(k))

    def out_g(k):
        return send_to(gs_ref.at[k], g_ref.at[0, k], gs_sem.at[k], gr_sem.at[k], peer(k))

    def pass_x(k):
        return send_to(x_ref.at[0, k], x_ref.at[1, k], xfs_sem.at[k], xfr_sem.at[k], partner)

    def pass_g(k):
        return send_to(g_ref.at[0, k], g_ref.at[1, k], gfs_sem.at[k], gfr_sem.at[k], partner)

    def across(index, k):
        return send_to(
            ysend_ref.at[index, k],
            yrecv_ref.at[index, k],
            ys_sem.at[index, k],
            yr_sem.at[index, k],
            partner,
        )

    def back(index, k):
        if index == 0:
            return send_to(xs_ref.at[k], res_out_ref.at[k], rs_sem.at[k], rr_sem.at[k], peer(k))
        return send_to(gs_ref.at[k], dx_out_ref.at[k], ds_sem.at[k], dr_sem.at[k], peer(k))

    def return_order(body):
        def step(j, carry):
            body(8 + 2 * j)
            body(4 + j)
            body(9 + 2 * j)
            return carry

        lax.fori_loop(0, 4, step, 0)
        for k in (2, 3, 1, 0):
            body(k)

    def turn_rows(source, target, m):
        target[:, pl.ds(pl.multiple_of(m * total, total), total)] = (
            source[m].reshape(total, width).T
        )

    def join(index, k):
        across(index, k).wait_recv()
        own = xs_ref if index == 0 else gs_ref
        own[k] = low(wide(own[k]) + wide(yrecv_ref[index, k]))
        back(index, k).start()

    def join_some(index, tile):
        join(index, 8 + 2 * tile)
        join(index, 4 + tile)
        join(index, 9 + 2 * tile)

    def join_last(index):
        for k in (2, 3, 1):
            join(index, k)
        across(index, 0).wait_recv()
        own, target = (xs_ref, res_out_ref) if index == 0 else (gs_ref, dx_out_ref)
        target[0] = low(wide(own[0]) + wide(yrecv_ref[index, 0]))

    greet_group(peers)
    here = pltpu.make_async_copy(weight_ref, w_ref.at[:, core], w_sem.at[0])
    here.start()
    there = send_to(weight_ref, w_ref.at[:, core], w_sem.at[1], w_sem.at[2], sibling)
    half = total // 2
    group = peers // 2

    def hits_of(part):
        ids = slot_ref[pl.ds(pl.multiple_of(part * half, half), half), 0:1]
        return [line_ref[m : m + 1, :] == ids for m in range(2)]

    def pack_x(part):
        hits = hits_of(part)
        onehot = low(jnp.where(hits[0] | hits[1], 1.0, 0.0))
        xs_ref[pl.ds(part * group, group)] = low(nn_dot(onehot, s2_ref[...])).reshape(
            group, rows, width
        )

        @pl.when(part == 0)
        def _():
            x_ref[0, 0] = xs_ref[0]
            pass_x(0).start()

        def launch(k):
            @pl.when(k > 0)
            def _():
                out_x(k).start()

        each(part * group, (part + 1) * group, launch)

    def pack_g(part):
        hits = hits_of(part)
        onehot = low(jnp.where(hits[0] | hits[1], 1.0, 0.0))
        gate = sum(
            jnp.sum(jnp.where(hits[m], line_ref[2 + m : 3 + m, :], 0.0), axis=1, keepdims=True)
            for m in range(2)
        )
        gs_ref[pl.ds(part * group, group)] = low(nn_dot(onehot, cot_ref[...]) * gate).reshape(
            group, rows, width
        )

        @pl.when(part == 0)
        def _():
            g_ref[0, 0] = gs_ref[0]

        def launch(k):
            @pl.when(k > 0)
            def _():
                out_g(k).start()

        each(part * group, (part + 1) * group, launch)

    each(0, 2, pack_x)
    there.start()
    each(0, 2, pack_g)

    def forward_x(k):
        out_x(k).wait_recv()
        pass_x(k).start()

    each(1, peers, forward_x)
    pass_g(0).start()
    here.wait()
    send_to(weight_ref, w_ref.at[:, 1 - core], w_sem.at[1], w_sem.at[2], sibling).wait_recv()
    there.wait_send()
    each(0, peers, lambda k: pass_x(k).wait_recv())

    def weights(which, lanes):
        return w_ref[:, :, :, pl.ds(pl.multiple_of(which * hidden + lanes, TILE), TILE)].reshape(
            width, TILE
        )

    acc_ref[...] = jnp.zeros_like(acc_ref)

    def forward_tile(tile, carry):
        lanes = pl.multiple_of(tile * TILE, TILE)
        here_lanes = pl.ds(lanes, TILE)

        def one_half(m):
            band = pl.ds(pl.multiple_of(m * total, total), total)
            x = x_ref[m].reshape(total, width)
            gate = nn_dot(x, weights(0, lanes))
            up = nn_dot(x, weights(1, lanes))
            gate_ref[band, here_lanes] = low(gate)
            up_ref[band, here_lanes] = low(up)
            act = low(gate / (1.0 + jnp.exp(-gate)) * up)
            act_ref[band, here_lanes] = act
            acc_ref[band, :] += nt_dot(act, weights(2, lanes))

        each(0, 2, one_half)

        def forward_g(k):
            @pl.when(k > 0)
            def _():
                out_g(k).wait_recv()
                pass_g(k).start()

        each(tile * (peers // tiles), (tile + 1) * (peers // tiles), forward_g)
        return carry

    lax.fori_loop(0, tiles, forward_tile, 0)
    each(1, peers, lambda k: out_x(k).wait_send())
    xs_ref[...] = low(acc_ref[:total, :]).reshape(peers, rows, width)
    ysend_ref[0] = low(acc_ref[total:, :]).reshape(peers, rows, width)
    return_order(lambda k: across(0, k).start())
    each(0, 2, lambda m: turn_rows(x_ref, xt_ref, m))
    acc_ref[...] = jnp.zeros_like(acc_ref)
    each(0, peers, lambda k: pass_g(k).wait_recv())

    def slope_tile(tile, carry):
        lanes = pl.multiple_of(tile * TILE, TILE)
        here_lanes = pl.ds(lanes, TILE)

        def one_half(m):
            band = pl.ds(pl.multiple_of(m * total, total), total)
            gate = wide(gate_ref[band, here_lanes])
            up = wide(up_ref[band, here_lanes])
            sig = 1.0 / (1.0 + jnp.exp(-gate))
            d_act = nn_dot(g_ref[m].reshape(total, width), weights(2, lanes))
            d_up = low(d_act * gate * sig)
            d_gate = low(d_act * up * sig * (1.0 + gate * (1.0 - sig)))
            gate_ref[band, here_lanes] = d_gate
            up_ref[band, here_lanes] = d_up
            acc_ref[band, :] += nt_dot(d_gate, weights(0, lanes)) + nt_dot(
                d_up, weights(1, lanes)
            )

        each(0, 2, one_half)
        join_some(0, tile)
        return carry

    lax.fori_loop(0, tiles, slope_tile, 0)
    join_last(0)
    each(1, peers, lambda k: out_g(k).wait_send())
    gs_ref[...] = low(acc_ref[:total, :]).reshape(peers, rows, width)
    ysend_ref[1] = low(acc_ref[total:, :]).reshape(peers, rows, width)
    return_order(lambda k: across(1, k).start())
    each(0, 2, lambda m: turn_rows(g_ref, gt_ref, m))

    def weight_tile(tile, carry):
        lanes = pl.multiple_of(tile * TILE, TILE)
        here_lanes = pl.ds(lanes, TILE)

        def keep(which, values):
            grads_ref[
                :, :, :, pl.ds(pl.multiple_of(which * hidden + lanes, TILE), TILE)
            ] = low(values).reshape(peers // 2, 2, rows, TILE)

        keep(0, nn_dot(xt_ref[...], gate_ref[:, here_lanes]))
        keep(1, nn_dot(xt_ref[...], up_ref[:, here_lanes]))
        keep(2, nn_dot(gt_ref[...], act_ref[:, here_lanes]))
        join_some(1, tile)
        return carry

    lax.fori_loop(0, tiles, weight_tile, 0)
    swap_grads = send_to(
        grads_ref.at[:, 1 - core], sibling_ref, grad_sem.at[0], grad_sem.at[1], sibling
    )
    swap_grads.start()
    join_last(1)
    each(0, peers, lambda k: pass_x(k).wait_send())
    each(0, peers, lambda k: pass_g(k).wait_send())
    for index in range(2):
        each(0, peers, lambda k: across(index, k).wait_send())
        each(1, peers, lambda k: back(index, k).wait_send())
    swap_grads.wait()
    grads_out_ref[...] = low(wide(grads_ref[:, core]) + wide(sibling_ref[...]))
    for index in range(2):
        each(1, peers, lambda k: back(index, k).wait_recv())


def run_expert(s2, cot, lines, slots, weights):
    length, width = s2.shape
    experts, shard, total = weights.shape
    peers = 2 * experts
    rows = slots.shape[0] // peers
    hidden = total // 3
    both = 2 * peers * rows
    vmem = pl.BlockSpec(memory_space=pltpu.VMEM)
    low_t, wide_t = jnp.bfloat16, jnp.float32
    dma = pltpu.SemaphoreType.DMA
    block = (peers, rows, width)
    return pl.pallas_call(
        expert_kernel,
        in_specs=[vmem] * 4 + [pl.BlockSpec(memory_space=pl.ANY)],
        out_specs=[vmem] * 3,
        out_shape=[
            jax.ShapeDtypeStruct(block, low_t),
            jax.ShapeDtypeStruct(block, low_t),
            jax.ShapeDtypeStruct(weights.shape, low_t),
        ],
        scratch_shapes=[
            pltpu.VMEM(block, low_t),
            pltpu.VMEM(block, low_t),
            pltpu.VMEM((2,) + block, low_t),
            pltpu.VMEM((2,) + block, low_t),
            pltpu.VMEM((experts, 2, shard, total), low_t),
            pltpu.VMEM((both, hidden), low_t),
            pltpu.VMEM((both, hidden), low_t),
            pltpu.VMEM((both, hidden), low_t),
            pltpu.VMEM((width, both), low_t),
            pltpu.VMEM((width, both), low_t),
            pltpu.VMEM((both, width), wide_t),
            pltpu.VMEM((experts, 2, shard, total), low_t),
            pltpu.VMEM((experts, shard, total), low_t),
            pltpu.VMEM((2,) + block, low_t),
            pltpu.VMEM((2,) + block, low_t),
            dma((3,)),
            dma((2,)),
        ]
        + [dma((peers,))] * 8
        + [dma((2, peers))] * 2
        + [dma((peers,))] * 4,
        compiler_params=pltpu.CompilerParams(
            collective_id=2, has_side_effects=True, vmem_limit_bytes=67043328
        ),
    )(s2, cot, lines, slots, weights)


def attend(
    hid_ref,
    token_block,
    weight,
    small_ref,
    gains,
    table_ref,
    s1_ref,
    qkv_ref,
    lse_ref,
    mixed_ref,
    mid_ref,
    s2_ref,
    tok_ref,
    line_ref,
    vt_ref,
    send_ref,
    recv_ref,
    send_sem,
    recv_sem,
    between,
):
    blocks = hid_ref.shape[0] // BLOCK
    heads_width = mixed_ref.shape[1]
    pairs = heads_width // PAIR
    gain_one, gain_two = gains
    lse_ref[...] = jnp.zeros_like(lse_ref)

    def copy(block):
        return to_partner(
            send_ref.at[block], recv_ref.at[block], send_sem.at[block], recv_sem.at[block]
        )

    def compute(block):
        rows = block_rows(block)
        source = wide(hid_ref[rows, :])
        s1 = low(source * lax.rsqrt(mean_last(source * source) + EPSILON) * gain_one)
        s1_ref[rows, :] = s1
        cosine, sine = spread_table(table_ref, block)
        for part in range(3):
            projected = nn_dot(s1, weight(part))
            for pair in range(pairs):
                chunk = projected[:, pair * PAIR : (pair + 1) * PAIR]
                if part < 2:
                    chunk = turn(chunk, cosine, sine)
                else:
                    vt_ref[pair * PAIR : (pair + 1) * PAIR, rows] = low(chunk.T)
                start = part * heads_width + pair * PAIR
                qkv_ref[rows, start : start + PAIR] = low(chunk)

        def one_pair(keys, pair):
            start = pl.multiple_of(pair * PAIR, PAIR)
            lanes = pl.ds(start, PAIR)
            key_lanes = pl.ds(pl.multiple_of(heads_width + start, PAIR), PAIR)
            query = qkv_ref[rows, lanes] * jnp.bfloat16(SCALING)
            key = qkv_ref[:keys, key_lanes]
            value_t = vt_ref[lanes, :keys]
            gathered = None
            for half in range(2):
                masked = jnp.where(head_lanes(query.shape, half, 1), query, jnp.bfloat16(0))
                scores = nt_dot(key, masked)
                highest = jnp.max(scores, axis=0, keepdims=True)
                expanded = jnp.exp(scores - highest)
                totals = jnp.sum(expanded, axis=0, keepdims=True)
                probs = low(expanded * (1.0 / totals))
                lse_ref[pl.ds(2 * pair + half, 1), rows] = highest + jnp.log(totals)
                found = nn_dot(value_t, probs)
                gathered = (
                    found
                    if half == 0
                    else jnp.where(head_lanes(found.shape, 1, 0), found, gathered)
                )
            mixed_ref[rows, lanes] = low(gathered.T)

        for static in range(blocks):

            @pl.when(block == static)
            def _():
                each(0, pairs, functools.partial(one_pair, (static + 1) * BLOCK))

        send_ref[block] = low(nt_dot(mixed_ref[rows, :], weight(3)))
        copy(block).start()

    def finish(block):
        rows = block_rows(block)
        copy(block).wait()
        mid = wide(hid_ref[rows, :]) + (wide(send_ref[block]) + wide(recv_ref[block]))
        mid_ref[rows, :] = mid
        s2 = low(mid * lax.rsqrt(mean_last(mid * mid) + EPSILON) * gain_two)
        s2_ref[rows, :] = s2
        tok = token_block(block)
        lane = lax.broadcasted_iota(jnp.int32, tok.shape, 1)
        logits = nn_dot(s2, small_ref[...]) + tok
        picked = [
            jnp.sum(
                jnp.where(wide(lane - ROUTER) == column(tok, ROUTE + member), logits, 0.0),
                axis=1,
                keepdims=True,
            )
            for member in range(2)
        ]
        gate = [
            1.0 / (1.0 + jnp.exp(picked[1 - member] - picked[member])) for member in range(2)
        ]
        tok = jnp.where(lane == GATE, gate[0], jnp.where(lane == GATE + 1, gate[1], tok))
        tok_ref[rows, :] = tok
        line_ref[:, rows] = tok.T[TARGET : TARGET + 8, :]

    each(0, blocks, compute)
    between()
    each(0, blocks, finish)


def forward_plain_kernel(
    hid_ref,
    tok_in_ref,
    block_ref,
    small_ref,
    rows_ref,
    table_ref,
    shard_ref,
    cot_own_ref,
    s1_ref,
    qkv_ref,
    lse_ref,
    mixed_ref,
    mid_ref,
    s2_ref,
    tok_ref,
    line_ref,
    expert_ref,
    cot_ref,
    vt_ref,
    send_ref,
    recv_ref,
    send_sem,
    recv_sem,
    wsend_sem,
    wrecv_sem,
    cot_sem,
):
    greet_group(2 * shard_ref.shape[0])
    own_rows = cot_own_ref.shape[0]
    heads_width = mixed_ref.shape[1]
    width = hid_ref.shape[1]
    mine = pl.ds(pl.multiple_of(lax.axis_index("tp") * own_rows, own_rows), own_rows)
    cot_copy = to_partner(cot_own_ref, cot_ref.at[mine], cot_sem.at[0], cot_sem.at[1])
    cot_copy.start()
    experts = CoreExchange(shard_ref, expert_ref, wsend_sem, wrecv_sem)
    experts.start()
    cot_ref[mine, :] = cot_own_ref[...]

    def weight(part):
        return block_ref[:, :, part * heads_width : (part + 1) * heads_width].reshape(
            width, heads_width
        )

    attend(
        hid_ref,
        lambda block: tok_in_ref[block_rows(block), :],
        weight,
        small_ref,
        (rows_ref[0:1, :], rows_ref[1:2, :]),
        table_ref,
        s1_ref,
        qkv_ref,
        lse_ref,
        mixed_ref,
        mid_ref,
        s2_ref,
        tok_ref,
        line_ref,
        vt_ref,
        send_ref,
        recv_ref,
        send_sem,
        recv_sem,
        lambda: None,
    )
    cot_copy.wait()
    experts.wait()


def forward_kernel(
    hid_own_ref,
    cot_own_ref,
    logit_ref,
    route_ref,
    rank_ref,
    drop_ref,
    gain_ref,
    router_ref,
    mixing_ref,
    value_ref,
    wqkv_ref,
    wout_ref,
    win_ref,
    wdown_ref,
    table_ref,
    all_out,
    small_ref,
    rows_ref,
    s1_out,
    qkv_out,
    lse_ref,
    mixed_out,
    mid_ref,
    s2_ref,
    tok_ref,
    line_ref,
    expert_ref,
    cot_out,
    all_ref,
    s1_ref,
    qkv_ref,
    mixed_ref,
    cot_ref,
    hid_ref,
    vt_ref,
    send_ref,
    recv_ref,
    shard_ref,
    stage_ref,
    small_all_ref,
    tok_all_ref,
    send_sem,
    recv_sem,
    wsend_sem,
    wrecv_sem,
    y_send,
    y_recv,
    up_send,
    up_recv,
    down_send,
    down_recv,
    x_send,
    x_recv,
    core_send,
    core_recv,
    store_sem,
):
    size, shard, _ = all_ref.shape
    planes = size // 4
    me = lax.axis_index("fsdp")
    tp = lax.axis_index("tp")
    z, x, core = me // 4, lax.rem(me // 2, 2), lax.rem(me, 2)
    own_rows, width = hid_own_ref.shape
    heads_width = wout_ref.shape[1]
    small_rows = shard // 2
    greet_group(size)
    partner = {"tp": 1 - tp}
    mine = pl.ds(pl.multiple_of(tp * own_rows, own_rows), own_rows)
    stage_ref[...] = jnp.zeros_like(stage_ref)
    stage_ref[0:2, :small_rows] = gain_ref[...]
    stage_ref[ROUTER:MIXING, :small_rows] = wide(router_ref[...])
    stage_ref[MIXING:VALUE, :small_rows] = wide(mixing_ref[...])
    stage_ref[VALUE : VALUE + 2, :small_rows] = wide(value_ref[...])
    small_all_ref[me, tp] = stage_ref[...].T[:small_rows, :]
    small_y = send_to(
        small_all_ref.at[me, tp], small_all_ref.at[me, tp], y_send.at[0], y_recv.at[0], partner
    )
    small_y.start()
    for part in range(3):
        all_ref[me, :, part * heads_width : (part + 1) * heads_width] = wqkv_ref[part]
    all_ref[me, :, 3 * heads_width :] = wout_ref[...]
    hid_y = send_to(hid_own_ref, hid_ref.at[mine], y_send.at[1], y_recv.at[1], partner)
    tok_y = send_to(tok_all_ref.at[tp], tok_all_ref.at[tp], y_send.at[2], y_recv.at[2], partner)
    cot_y = send_to(cot_own_ref, cot_ref.at[mine], y_send.at[3], y_recv.at[3], partner)
    experts = CoreExchange(shard_ref, expert_ref, wsend_sem, wrecv_sem)
    expert_count, _, hidden = wdown_ref.shape

    def stage_tokens():
        tok_all_ref[tp] = jnp.zeros(tok_all_ref.shape[1:], jnp.float32)
        routes = route_ref[...]
        kept = jnp.logical_and(routes < expert_count, drop_ref[...] == 0)
        target = jnp.where(kept, routes * (own_rows * 2 * 9 // 48) + rank_ref[...], -1)
        tok_all_ref[tp, ROUTER:MIXING, :] = logit_ref[...]
        tok_all_ref[tp, ROUTE : ROUTE + 2, :] = wide(routes)
        tok_all_ref[tp, TARGET : TARGET + 2, :] = wide(target)

    def stage_shard():
        def one(e):
            for part in range(2):
                shard_ref[e, :, part * hidden : (part + 1) * hidden] = win_ref[e, :, part, :]
            shard_ref[e, :, 2 * hidden :] = wdown_ref[e]

        each(0, expert_count, one)

    def number(plane, line):
        return plane * 4 + line * 2 + core

    def piece(kind, number_of, send, recv, slot, device):
        array = small_all_ref if kind else all_ref
        return send_to(
            array.at[number_of],
            array.at[number_of],
            send.at[kind, slot],
            recv.at[kind, slot],
            device,
        )

    def up(kind, step, plane):
        device = {"fsdp": number(lax.min(z + 1, planes - 1), x)}
        return piece(kind, number(plane, x), up_send, up_recv, step, device)

    def down(kind, step, plane):
        device = {"fsdp": number(lax.max(z - 1, 0), x)}
        return piece(kind, number(plane, x), down_send, down_recv, step, device)

    def side(kind, plane, line):
        device = {"fsdp": number(z, 1 - x)}
        return piece(kind, number(plane, line), x_send, x_recv, plane, device)

    def sibling(kind, plane, line, parity):
        return piece(
            kind,
            plane * 4 + line * 2 + parity,
            core_send,
            core_recv,
            plane * 2 + line,
            {"fsdp": me + 1 - 2 * core},
        )

    def launch(kind):
        @pl.when(z < planes - 1)
        def _():
            up(kind, 0, z).start()

        @pl.when(z > 0)
        def _():
            down(kind, 0, z).start()

        side(kind, z, x).start()
        sibling(kind, z, x, core).start()

    launch(0)
    hid_y.start()
    stage_tokens()
    tok_y.start()
    cot_y.start()
    hid_ref[mine, :] = hid_own_ref[...]
    cot_ref[mine, :] = cot_own_ref[...]
    small_y.wait()
    launch(1)
    stage_shard()
    for step in range(1, planes):
        for kind in range(2):

            @pl.when(z >= step)
            def _():
                up(kind, step - 1, z - step).wait_recv()

                @pl.when(z < planes - 1)
                def _():
                    up(kind, step, z - step).start()

                side(kind, z - step, x).start()
                sibling(kind, z - step, x, core).start()

            @pl.when(z + step < planes)
            def _():
                down(kind, step - 1, z + step).wait_recv()

                @pl.when(z > 0)
                def _():
                    down(kind, step, z + step).start()

                side(kind, z + step, x).start()
                sibling(kind, z + step, x, core).start()

    experts.start()
    for step in range(planes):
        for kind in range(2):

            @pl.when(z >= step)
            def _():
                side(kind, z - step, 1 - x).wait_recv()
                sibling(kind, z - step, 1 - x, core).start()

            if step > 0:

                @pl.when(z + step < planes)
                def _():
                    side(kind, z + step, 1 - x).wait_recv()
                    sibling(kind, z + step, 1 - x, core).start()

    for plane in range(planes):
        for line in range(2):
            for kind in range(2):
                sibling(kind, plane, line, 1 - core).wait_recv()
    small_all = small_all_ref[...].reshape(width, PAIR)
    small_ref[...] = low(small_all)
    rows_ref[...] = small_all.T[:8, :]
    tok_y.wait()
    hid_y.wait()

    def token_block(block):
        per = own_rows // BLOCK
        lanes = pl.ds(pl.multiple_of(lax.rem(block, per) * BLOCK, BLOCK), BLOCK)
        part = tok_all_ref[block // per, :, lanes]
        blank = jnp.zeros((PAIR - part.shape[0], BLOCK), jnp.float32)
        return jnp.concatenate([part, blank], axis=0).T

    def weight(part):
        return all_ref[:, :, part * heads_width : (part + 1) * heads_width].reshape(
            width, heads_width
        )

    stores = [
        pltpu.make_async_copy(source, target, store_sem.at[index])
        for index, (source, target) in enumerate(
            [
                (all_ref, all_out),
                (s1_ref, s1_out),
                (qkv_ref, qkv_out),
                (mixed_ref, mixed_out),
                (cot_ref, cot_out),
            ]
        )
    ]
    stores[0].start()

    def between():
        for store in stores[1:4]:
            store.start()
        cot_y.wait()
        stores[4].start()

    attend(
        hid_ref,
        token_block,
        weight,
        small_ref,
        (rows_ref[0:1, :], rows_ref[1:2, :]),
        table_ref,
        s1_ref,
        qkv_ref,
        lse_ref,
        mixed_ref,
        mid_ref,
        s2_ref,
        tok_ref,
        line_ref,
        vt_ref,
        send_ref,
        recv_ref,
        send_sem,
        recv_sem,
        between,
    )
    for kind in range(2):
        for step in range(planes):

            @pl.when(jnp.logical_and(z >= step, z < planes - 1))
            def _():
                up(kind, step, z - step).wait_send()

            @pl.when(jnp.logical_and(z + step < planes, z > 0))
            def _():
                down(kind, step, z + step).wait_send()

        for plane in range(planes):
            side(kind, plane, x).wait_send()
            for line in range(2):
                sibling(kind, plane, line, core).wait_send()
    for store in stores:
        store.wait()
    experts.wait()


def backward_kernel(
    res_ref,
    dx_ref,
    slot_ref,
    tok_ref,
    cot_ref,
    mid_hbm,
    s1_hbm,
    qkv_hbm,
    lse_ref,
    mixed_hbm,
    block_hbm,
    small_ref,
    rows_ref,
    table_ref,
    own_ref,
    egrad_ref,
    grad_ref,
    base_ref,
    other_ref,
    big_ref,
    arrived_ref,
    gsend_ref,
    grecv_ref,
    ssend_ref,
    srecv_ref,
    mid_ref,
    s1_ref,
    qkv_ref,
    mixed_ref,
    block_ref,
    hsend_ref,
    hrecv_ref,
    gmid_ref,
    gown_ref,
    kt_ref,
    gm_ref,
    dk_ref,
    dv_ref,
    gp_ref,
    att_ref,
    s2_ref,
    slope_ref,
    value_ref,
    acc_gain_ref,
    gsend_sem,
    grecv_sem,
    hsend_sem,
    hrecv_sem,
    esend_sem,
    erecv_sem,
    ssend_sem,
    srecv_sem,
    load_sem,
):
    loads = [
        pltpu.make_async_copy(source, target, load_sem.at[index])
        for index, (source, target) in enumerate(
            [
                (mid_hbm, mid_ref),
                (qkv_hbm, qkv_ref),
                (mixed_hbm, mixed_ref),
                (block_hbm, block_ref),
                (s1_hbm, s1_ref),
            ]
        )
    ]
    for load in loads:
        load.start()
    greet_group(2 * egrad_ref.shape[0])
    experts = CoreExchange(egrad_ref, arrived_ref, esend_sem, erecv_sem)
    tp = lax.axis_index("tp")
    width = dx_ref.shape[1]
    blocks = cot_ref.shape[0] // BLOCK
    heads_width = mixed_ref.shape[1]
    pairs = heads_width // PAIR
    gain_one = rows_ref[0:1, :]
    gain_two = rows_ref[1:2, :]
    slot_row = slot_ref[0:1, :]

    def weights(first_part, last_part):
        lanes = slice(first_part * heads_width, last_part * heads_width)
        return block_ref[:, :, lanes].reshape(width, (last_part - first_part) * heads_width)

    half_blocks = blocks // 2
    experts.start()

    def row_copy(block):
        return to_partner(
            gsend_ref.at[block], grecv_ref.at[block], gsend_sem.at[block], grecv_sem.at[block]
        )

    def share_copy(block):
        return to_partner(
            ssend_ref.at[block], srecv_ref.at[block], ssend_sem.at[block], srecv_sem.at[block]
        )

    def stream_copy(slot):
        return to_partner(
            hsend_ref.at[slot], hrecv_ref.at[slot], hsend_sem.at[slot], hrecv_sem.at[slot]
        )

    def slab_of(block):
        return block_rows(lax.rem(block, half_blocks))

    def backwards(body):
        each(0, blocks, lambda step: body(blocks - 1 - step))

    def send_rows(block):
        rows = block_rows(block)
        tok = tok_ref[rows, :]
        onehots = [low(jnp.where(column(tok, TARGET + m) == slot_row, 1.0, 0.0)) for m in range(2)]
        gsend_ref[block] = low(nn_dot(onehots[0] + onehots[1], dx_ref[...]))
        row_copy(block).start()
        placed = [nn_dot(onehot, res_ref[...]) for onehot in onehots]
        cot_wide = wide(cot_ref[rows, :])
        shares = [
            column(tok, GATE + m) * jnp.sum(placed[m] * cot_wide, axis=1, keepdims=True)
            for m in range(2)
        ]
        ssend_ref[block] = lane_matrix(tok.shape, [(0, shares[0]), (1, shares[1])]).T[:8, :]
        share_copy(block).start()
        mixture = column(tok, GATE) * placed[0] + column(tok, GATE + 1) * placed[1]

        @pl.when(tp == block // half_blocks)
        def _():
            base_ref[slab_of(block), :] = mixture

        @pl.when(tp != block // half_blocks)
        def _():
            other_ref[slab_of(block), :] = low(mixture)

    backwards(send_rows)
    for load in loads:
        load.wait()
    kt_ref[...] = qkv_ref[:, heads_width : 2 * heads_width].T
    dk_ref[...] = jnp.zeros_like(dk_ref)
    dv_ref[...] = jnp.zeros_like(dv_ref)
    acc_gain_ref[...] = jnp.zeros_like(acc_gain_ref)

    def main(block):
        rows = block_rows(block)
        mine = tp == block // half_blocks
        mine_f = jnp.where(mine, 1.0, 0.0)
        mid = mid_ref[rows, :]
        cot = cot_ref[rows, :]
        cot_wide = wide(cot)
        tok = tok_ref[rows, :]
        scale = lax.rsqrt(mean_last(mid * mid) + EPSILON)
        unit = mid * scale
        normed = unit * gain_two
        s2 = low(normed)
        small = small_ref[...]
        mixing = nn_dot(s2, small)
        value_dot = nn_dot(cot, small)
        normed_dot = jnp.sum(normed * cot_wide, axis=1, keepdims=True)
        route = [column(tok, ROUTE + member) for member in range(2)]
        gate = [column(tok, GATE + member) for member in range(2)]

        def weight_of(expert):
            return sum(jnp.where(route[m] == expert, gate[m], 0.0) for m in range(2))

        copy_weight = weight_of(COPY)
        copy_share = [jnp.where(route[m] == COPY, normed_dot, 0.0) for m in range(2)]
        alpha = copy_weight
        columns = []
        value_columns = []
        for c in range(2):
            weight = weight_of(COPY + 1 + c)
            left = column(mixing, MIXING + 2 * c)
            right = column(mixing, MIXING + 2 * c + 1)
            a0 = 1.0 / (1.0 + jnp.exp(right - left))
            a1 = 1.0 / (1.0 + jnp.exp(left - right))
            vd = column(value_dot, VALUE + c)
            alpha = alpha + weight * a0
            for m in range(2):
                copy_share[m] = copy_share[m] + jnp.where(
                    route[m] == COPY + 1 + c, a0 * normed_dot + a1 * vd, 0.0
                )
            slope = a0 * a1 * weight * (normed_dot - vd)
            columns.append((MIXING + 2 * c, slope))
            columns.append((MIXING + 2 * c + 1, -slope))
            value_columns.append((VALUE + c, weight * a1))
        value_matrix = lane_matrix(tok.shape, value_columns)
        base = mid + alpha * normed + nt_dot(low(value_matrix), small)

        @pl.when(mine)
        def _():
            base_ref[slab_of(block), :] += base

        row_copy(block).wait()
        share_copy(block).wait()
        extra = ssend_ref[block] + srecv_ref[block]
        extra = jnp.concatenate(
            [extra, jnp.zeros((PAIR - extra.shape[0], BLOCK), jnp.float32)], axis=0
        ).T
        share = [column(extra, m) + gate[m] * copy_share[m] for m in range(2)]
        lane = lax.broadcasted_iota(jnp.int32, tok.shape, 1)
        slopes = lane_matrix(tok.shape, columns)
        for m in range(2):
            local = share[m] - gate[m] * (share[0] + share[1])
            slopes = slopes + jnp.where(wide(lane - ROUTER) == route[m], local, 0.0)
        slopes_low = low(slopes)
        grad_normed = (
            wide(gsend_ref[block])
            + wide(grecv_ref[block])
            + alpha * cot_wide
            + nt_dot(slopes_low, small)
        )
        s2_ref[rows, :] = s2
        slope_ref[rows, :] = low(slopes * mine_f)
        value_ref[rows, :] = low(value_matrix * mine_f)
        gain_grad = jnp.sum(unit * grad_normed, axis=0, keepdims=True) * mine_f
        acc_gain_ref[...] += jnp.broadcast_to(gain_grad, acc_gain_ref.shape)
        scaled = grad_normed * gain_two
        grad_mid = cot_wide + scale * (scaled - unit * mean_last(scaled * unit))
        gmid_ref[rows, :] = grad_mid
        attended = low(grad_mid)
        att_ref[rows, :] = attended
        gm_ref[...] = low(nn_dot(attended, weights(3, 4)))
        cosine, sine = spread_table(table_ref, block)

        def one_pair(keys, pair):
            start = pl.multiple_of(pair * PAIR, PAIR)
            lanes = pl.ds(start, PAIR)
            key_lanes = pl.ds(pl.multiple_of(heads_width + start, PAIR), PAIR)
            value_lanes = pl.ds(pl.multiple_of(2 * heads_width + start, PAIR), PAIR)
            query = qkv_ref[rows, lanes] * jnp.bfloat16(SCALING)
            key = qkv_ref[:keys, key_lanes]
            value = qkv_ref[:keys, value_lanes]
            grad_out = gm_ref[:, lanes]
            key_t = kt_ref[lanes, :keys]
            grad_value = None
            for half in range(2):
                keep = head_lanes(query.shape, half, 1)
                q_half = jnp.where(keep, query, jnp.bfloat16(0))
                g_half = jnp.where(keep, grad_out, jnp.bfloat16(0))
                probs = jnp.exp(nt_dot(key, q_half) - lse_ref[pl.ds(2 * pair + half, 1), rows])
                grad_probs = nt_dot(value, g_half)
                inner = jnp.sum(probs * grad_probs, axis=0, keepdims=True)
                grad_scores = low(probs * (grad_probs - inner))
                value_part = nn_dot(low(probs), g_half)
                key_part = nn_dot(grad_scores, q_half)
                query_part = nn_dot(key_t, grad_scores)
                if half == 0:
                    grad_value, grad_key, grad_query = value_part, key_part, query_part
                else:
                    grad_value = grad_value + value_part
                    grad_key = grad_key + key_part
                    grad_query = jnp.where(
                        head_lanes(query_part.shape, 1, 0), query_part, grad_query
                    )
            dv_ref[:keys, lanes] += grad_value
            dk_ref[:keys, lanes] += grad_key
            gp_ref[rows, lanes] = low(turn(grad_query.T * SCALING, cosine, -sine))
            gp_ref[rows, key_lanes] = low(turn(dk_ref[rows, lanes], cosine, -sine))
            gp_ref[rows, value_lanes] = low(dv_ref[rows, lanes])

        for static in range(blocks):

            @pl.when(block == static)
            def _():
                each(0, pairs, functools.partial(one_pair, (static + 1) * BLOCK))

        stream_grad = nt_dot(gp_ref[rows, :], weights(0, 3))
        slot = lax.rem(block, half_blocks)

        @pl.when(mine)
        def _():
            gown_ref[slot] = stream_grad

        @pl.when(jnp.logical_not(mine))
        def _():
            hsend_ref[slot] = low(stream_grad)
            stream_copy(slot).start()

    backwards(main)
    s1_turned = s1_ref[...].T
    for part in range(3):
        lanes = slice(part * heads_width, (part + 1) * heads_width)
        big_ref[:, lanes] = low(nn_dot(s1_turned, gp_ref[:, lanes]))
    big_ref[:, 3 * heads_width : 4 * heads_width] = low(tn_dot(att_ref[...], mixed_ref[...]))
    tall = jnp.where(
        lax.broadcasted_iota(jnp.int32, (PAIR, width), 0) == 1,
        jnp.broadcast_to(acc_gain_ref[0:1, :], (PAIR, width)),
        0.0,
    )
    big_ref[:, 4 * heads_width :] = low(
        tn_dot(s2_ref[...], slope_ref[...]) + tn_dot(cot_ref[...], value_ref[...]) + tall.T
    )
    for slot in reversed(range(half_blocks)):
        slab = slice(slot * BLOCK, (slot + 1) * BLOCK)
        stream_copy(slot).wait()
        source = wide(own_ref[slab, :])
        scale = lax.rsqrt(mean_last(source * source) + EPSILON)
        unit = source * scale
        scaled = (gown_ref[slot] + wide(hrecv_ref[slot])) * gain_one
        mid_rows = block_rows(tp * half_blocks + slot)
        grad_ref[slab, :] = gmid_ref[mid_rows, :] + scale * (
            scaled - unit * mean_last(scaled * unit)
        )
    experts.wait()


def forward_results(length, width, heads_width, shard):
    low_t, wide_t = jnp.bfloat16, jnp.float32
    return [
        jax.ShapeDtypeStruct((length, width), low_t),
        jax.ShapeDtypeStruct((length, 3 * heads_width), low_t),
        jax.ShapeDtypeStruct((8, length), wide_t),
        jax.ShapeDtypeStruct((length, heads_width), low_t),
        jax.ShapeDtypeStruct((length, width), wide_t),
        jax.ShapeDtypeStruct((length, width), low_t),
        jax.ShapeDtypeStruct((length, PAIR), wide_t),
        jax.ShapeDtypeStruct((8, length), wide_t),
        jax.ShapeDtypeStruct(shard, low_t),
        jax.ShapeDtypeStruct((length, width), low_t),
    ]


def attend_scratch(length, width, heads_width):
    blocks = length // BLOCK
    return [
        pltpu.VMEM((heads_width, length), jnp.bfloat16),
        pltpu.VMEM((blocks, BLOCK, width), jnp.bfloat16),
        pltpu.VMEM((blocks, BLOCK, width), jnp.bfloat16),
    ]


def run_forward_plain(hid, tok, blocks, small, rows, table, shard, cot):
    length, width = hid.shape
    heads_width = blocks.shape[2] // 4
    vmem = pl.BlockSpec(memory_space=pltpu.VMEM)
    dma = pltpu.SemaphoreType.DMA
    count = length // BLOCK
    return pl.pallas_call(
        forward_plain_kernel,
        in_specs=[vmem] * 8,
        out_specs=[vmem] * 10,
        out_shape=forward_results(length, width, heads_width, shard.shape),
        scratch_shapes=attend_scratch(length, width, heads_width)
        + [dma((count,)), dma((count,)), dma((shard.shape[0],)), dma((shard.shape[0],)), dma((2,))],
        compiler_params=pltpu.CompilerParams(
            collective_id=0, has_side_effects=True, vmem_limit_bytes=60 << 20
        ),
    )(hid, tok, blocks, small, rows, table, shard, cot)


def run_forward(*operands):
    hid, wout, wdown, table = operands[0], operands[11], operands[13], operands[14]
    own_rows, width = hid.shape
    length = 2 * table.shape[0]
    shard, heads_width = wout.shape
    experts, _, hidden = wdown.shape
    size = lax.axis_size("fsdp")
    count = length // BLOCK
    hbm = pl.BlockSpec(memory_space=pl.ANY)
    vmem = pl.BlockSpec(memory_space=pltpu.VMEM)
    low_t, wide_t = jnp.bfloat16, jnp.float32
    dma = pltpu.SemaphoreType.DMA
    return pl.pallas_call(
        forward_kernel,
        in_specs=[vmem] * 15,
        out_specs=[hbm, vmem, vmem, hbm, hbm, vmem, hbm]
        + [vmem] * 4
        + [hbm, hbm],
        out_shape=[
            jax.ShapeDtypeStruct((size, shard, 4 * heads_width), low_t),
            jax.ShapeDtypeStruct((width, PAIR), low_t),
            jax.ShapeDtypeStruct((8, width), wide_t),
        ]
        + forward_results(length, width, heads_width, (experts, shard, 3 * hidden)),
        scratch_shapes=[
            pltpu.VMEM((size, shard, 4 * heads_width), low_t),
            pltpu.VMEM((length, width), low_t),
            pltpu.VMEM((length, 3 * heads_width), low_t),
            pltpu.VMEM((length, heads_width), low_t),
            pltpu.VMEM((length, width), low_t),
            pltpu.VMEM((length, width), low_t),
        ]
        + attend_scratch(length, width, heads_width)
        + [
            pltpu.VMEM((experts, shard, 3 * hidden), low_t),
            pltpu.VMEM((PAIR, PAIR), wide_t),
            pltpu.VMEM((size, 2, shard // 2, PAIR), wide_t),
            pltpu.VMEM((2, 32, own_rows), wide_t),
            dma((count,)),
            dma((count,)),
            dma((experts,)),
            dma((experts,)),
            dma((4,)),
            dma((4,)),
        ]
        + [dma((2, size // 4))] * 6
        + [dma((2, size // 2))] * 2
        + [dma((5,))],
        compiler_params=pltpu.CompilerParams(
            collective_id=3, has_side_effects=True, vmem_limit_bytes=60 << 20
        ),
    )(*operands)


def run_backward(*operands):
    cot, mid, s1, qkv, mixed, blocks, own, egrads = (
        operands[index] for index in (4, 5, 6, 7, 9, 10, 14, 15)
    )
    length, width = cot.shape
    heads_width = mixed.shape[1]
    count = length // BLOCK
    own_rows = own.shape[0]
    vmem = pl.BlockSpec(memory_space=pltpu.VMEM)
    hbm = pl.BlockSpec(memory_space=pl.ANY)
    low_t, wide_t = jnp.bfloat16, jnp.float32
    dma = pltpu.SemaphoreType.DMA
    return pl.pallas_call(
        backward_kernel,
        in_specs=[vmem] * 5
        + [hbm] * 3
        + [vmem]
        + [hbm] * 2
        + [vmem] * 4
        + [hbm],
        out_specs=[vmem] * 4 + [hbm],
        out_shape=[
            jax.ShapeDtypeStruct((own_rows, width), wide_t),
            jax.ShapeDtypeStruct((own_rows, width), wide_t),
            jax.ShapeDtypeStruct((own_rows, width), low_t),
            jax.ShapeDtypeStruct((width, 4 * heads_width + PAIR), low_t),
            jax.ShapeDtypeStruct(egrads.shape, low_t),
        ],
        scratch_shapes=[
            pltpu.VMEM((count, BLOCK, width), low_t),
            pltpu.VMEM((count, BLOCK, width), low_t),
            pltpu.VMEM((count, 8, BLOCK), wide_t),
            pltpu.VMEM((count, 8, BLOCK), wide_t),
            pltpu.VMEM(mid.shape, wide_t),
            pltpu.VMEM(s1.shape, low_t),
            pltpu.VMEM(qkv.shape, low_t),
            pltpu.VMEM(mixed.shape, low_t),
            pltpu.VMEM(blocks.shape, low_t),
            pltpu.VMEM((2, BLOCK, width), low_t),
            pltpu.VMEM((2, BLOCK, width), low_t),
            pltpu.VMEM((length, width), wide_t),
            pltpu.VMEM((2, BLOCK, width), wide_t),
            pltpu.VMEM((heads_width, length), low_t),
            pltpu.VMEM((BLOCK, heads_width), low_t),
            pltpu.VMEM((length, heads_width), wide_t),
            pltpu.VMEM((length, heads_width), wide_t),
            pltpu.VMEM((length, 3 * heads_width), low_t),
            pltpu.VMEM((length, width), low_t),
            pltpu.VMEM((length, width), low_t),
            pltpu.VMEM((length, PAIR), low_t),
            pltpu.VMEM((length, PAIR), low_t),
            pltpu.VMEM((8, width), wide_t),
            dma((count,)),
            dma((count,)),
            dma((2,)),
            dma((2,)),
            dma((egrads.shape[0],)),
            dma((egrads.shape[0],)),
            dma((count,)),
            dma((count,)),
            dma((5,)),
        ],
        compiler_params=pltpu.CompilerParams(
            collective_id=1, has_side_effects=True, vmem_limit_bytes=60 << 20
        ),
    )(*operands)


def shards(
    hidden,
    prev_logits,
    routes,
    slot_rank,
    dropped,
    cotangent,
    attn_norm,
    ffn_norm,
    w_qkv,
    w_attn_out,
    w_router,
    w_const_gate,
    w_const_value,
    w_expert_in,
    w_expert_out,
):
    own_rows, width = hidden.shape
    length = own_rows * lax.axis_size("tp")
    experts = w_expert_in.shape[0]
    route_count = w_router.shape[1]
    capacity = 9 * length // (4 * route_count)
    planned = lax.axis_size("fsdp") == 16
    table = jnp.asarray(rotary_table(length))
    gains = jnp.stack([wide(attn_norm), wide(ffn_norm)], axis=0)
    wqkv = w_qkv.transpose(1, 0, 2)
    operands = (
        hidden,
        cotangent,
        prev_logits.T,
        routes.T,
        slot_rank.T,
        dropped.T,
        gains,
        w_router.T,
        w_const_gate.T,
        w_const_value.T,
        wqkv,
        w_attn_out,
        w_expert_in,
        w_expert_out,
    )
    if planned:
        forward = run_forward(*operands, table)
    else:
        forward = forward_plain(operands, table)
    blocks, small, rows, s1, qkv, lse, mixed, mid, s2, tok, lines, gathered, cot = forward
    expert_weights = join_weights(gathered, experts)
    peers = 2 * experts
    half = capacity // 2
    block = half // 2
    place = jnp.arange(peers * block)
    owner = (lax.axis_index("fsdp") % peers) ^ (place // block)
    slot = wide(
        (owner // 2) * capacity
        + lax.axis_index("tp") * half
        + (owner % 2) * block
        + place % block
    )
    results, grad_rows, grads_exp = run_expert(
        s2, cot, lines, jnp.broadcast_to(slot[:, None], (slot.shape[0], PAIR)), expert_weights
    )
    grad_hidden, base, for_other, big, arrived = run_backward(
        results.reshape(-1, width),
        grad_rows.reshape(-1, width),
        jnp.broadcast_to(slot[None, :], (8, slot.shape[0])),
        tok,
        cot,
        mid,
        s1,
        qkv,
        lse,
        mixed,
        blocks,
        small,
        rows,
        table,
        hidden,
        split_grads(grads_exp),
    )
    received, red, last = (run_finish if planned else finish_plain)(big, wqkv, for_other)
    output, grad_hidden, grad_qkv, grad_attn_out, gain_grads, grad_router, grad_mixing, grad_value, grad_in, grad_out = run_write(
        base, received, grad_hidden, red, last, gains, arrived
    )
    return (
        output,
        grad_hidden,
        gain_grads[0],
        gain_grads[1],
        grad_qkv.transpose(1, 0, 2),
        grad_attn_out,
        grad_router.T,
        grad_mixing.T,
        grad_value.T,
        grad_in,
        grad_out,
    )


def solution(mesh):
    in_specs = (
        P(("fsdp", "tp"), None),
        P(("fsdp", "tp"), None),
        P(("fsdp", "tp"), None),
        P(("fsdp", "tp"), None),
        P(("fsdp", "tp"), None),
        P(("fsdp", "tp"), None),
        P(("fsdp", "tp")),
        P(("fsdp", "tp")),
        P("fsdp", None, "tp"),
        P("fsdp", "tp"),
        P(("fsdp", "tp"), None),
        P(("fsdp", "tp"), None),
        P(("fsdp", "tp"), None),
        P(None, "fsdp", None, "tp"),
        P(None, "fsdp", "tp"),
    )
    out_specs = (
        P(("fsdp", "tp"), None),
        P(("fsdp", "tp"), None),
        P(("fsdp", "tp")),
        P(("fsdp", "tp")),
        P("fsdp", None, "tp"),
        P("fsdp", "tp"),
        P(("fsdp", "tp"), None),
        P(("fsdp", "tp"), None),
        P(("fsdp", "tp"), None),
        P(None, "fsdp", None, "tp"),
        P(None, "fsdp", "tp"),
    )
    return jax.shard_map(shards, mesh=mesh, in_specs=in_specs, out_specs=out_specs, check_vma=False)
```

profile of v0, /device:TPU:12, one launch (start us, length us, event | category | flops | bytes accessed | tf_op | source)
XLA Modules:
  0.0 318.0 jit_solution(5960295703884847084)
XLA Ops:
  0.7 1.3 maximum_convert_fusion.gain_ref
  2.0 0.6 broadcast_in_dim.5.slot_ref
  2.6 0.9 broadcast_in_dim.4.slot_ref
  3.5 80.7 %shard_map.239 = (bf16[16,48,1536]{2,1,0:T(8,128)(2,1)}, bf16[768,128]{1,0:T(8,128)(2,1)}, f32[8,768]{1,0:T(8,128)}, bf16[1024,768]{1,0:T(8,128)(2,1)}, bf16[102...) custom-call(bf16[512,768]{1,0:T(8,128)(2,1)} %own_ref.1, ...), custom_call_target="tpu_custom_call" | custom-call | tf_op jit(solution)/shard_map/pallas_call | solution.py:1791
  84.2 133.7 %shard_map.240 = (bf16[16,48,768]{2,1,0:T(8,128)(2,1)}, bf16[16,48,768]{2,1,0:T(8,128)(2,1)}, bf16[8,48,3072]{2,1,0:T(8,128)(2,1)}) custom-call(bf16[1024,768]{1,0:T(8,128)(2,1)} %get-tuple-element.45.s2_ref, bf16[1024,768]{1,0:T(8,128)(2,1)} %get-tuple-element.46.cot_ref, f32[8,1024]{1,0:T(8,128)} %get-tuple-element.47.line_ref, ...), custom_call_target="tpu_custom_call" | custom-call | tf_op jit(solution)/shard_map/pallas_call | solution.py:924
  217.9 60.7 %shard_map.241 = (f32[512,768]{1,0:T(8,128)}, f32[512,768]{1,0:T(8,128)}, bf16[512,768]{1,0:T(8,128)(2,1)}, bf16[768,1664]{1,0:T(8,128)(2,1)}, bf16[8,48,3072]{2,1,0:T(8,128)(2,1)}) custom-call(bf16[768,768]{1,0:T(8,128)(2,1)} %bitcast.22, bf16[768,768]{1,0:T(8,128)(2,1)} %bitcast.23, f32[8,768]{1,0:T(8,128)} %broadcast_in_dim.5.slot_ref, ...), custom_call_target="tpu_custom_call" | custom-call | tf_op jit(solution)/shard_map/pallas_call | solution.py:1845
  278.7 29.4 %shard_map.242 = (bf16[512,768]{1,0:T(8,128)(2,1)}, f32[48,1536]{1,0:T(8,128)}, f32[24,128]{1,0:T(8,128)}) custom-call(bf16[16,48,1664]{2,1,0:T(8,128)(2,1)} %bitcast.21, bf16[3,48,384]{2,1,0:T(8,128)(2,1)} %bitcast.25, bf16[512,768]{1,0:T(8,128)(2,1)} %get-tuple-element.63.other_ref), custom_call_target="tpu_custom_call" | custom-call | tf_op jit(solution)/shard_map/pallas_call | solution.py:499
  308.0 8.7 %shard_map.243 = (bf16[512,768]{1,0:T(8,128)(2,1)}, f32[512,768]{1,0:T(8,128)}, f32[3,48,384]{2,1,0:T(8,128)}, f32[48,384]{1,0:T(8,128)}, f32[2,24]{1,0:T(2,128)...) custom-call(f32[512,768]{1,0:T(8,128)} %get-tuple-element.61.base_re, ...), custom_call_target="tpu_custom_call" | custom-call | tf_op jit(solution)/shard_map/pallas_call | solution.py:586
  316.7 1.2 slice_bitcast_fusion
  (1 shorter events, 0.0 us)
where the time goes:
time: 322 us; the launch traced here: 318 us
  Pallas kernels  313 us (97%)
    pallas_call x1, Pallas kernels, run_expert(): pl.pallas_call(expert_kernel, in_specs=[vmem] * 4 + [pl.BlockSpec(memory_...  134 us
    pallas_call x1, Pallas kernels, run_forward(): pl.pallas_call(forward_kernel, in_specs=[vmem] * 15, out_specs=[hbm, vmem...  80.7 us
    pallas_call x1, Pallas kernels, run_backward(): pl.pallas_call(backward_kernel, in_specs=[vmem] * 5 + [hbm] * 3 + [vmem]...  60.7 us
    pallas_call x1, Pallas kernels, run_finish(): pl.pallas_call(finish_kernel, in_specs=[vmem] * 3, out_specs=[vmem] * 3,...  29.4 us
    pallas_call x1, Pallas kernels, run_write(): pl.pallas_call(write_kernel, grid=(experts,), in_specs=[rows, rows, rows,...  8.68 us

commit v1 on v0

--- a/solution.py
+++ b/solution.py
@@ -26,6 +26,7 @@
 
 
 TILE = 256
+SUB = 16
 
 
 def swap(values):
@@ -304,9 +305,11 @@
         self.experts, self.copy, self.arrival = experts, copy, arrival
         self.local = pltpu.make_async_copy(source.at[mine], target.at[mine], send_sem.at[0])
 
-    def start(self):
+    def start(self, done=()):
         self.local.start()
-        each(1, self.experts, lambda k: self.copy(k).start())
+        for k in range(1, self.experts):
+            if k not in done:
+                self.copy(k).start()
 
     def wait(self):
         each(1, self.experts, lambda k: self.copy(k).wait_send())
@@ -314,7 +317,7 @@
         self.local.wait()
 
 
-def finish_kernel(
+def sum_stages(
     big_ref,
     wqkv_ref,
     other_ref,
@@ -343,12 +346,12 @@
     y_recv,
 ):
     size = big_ref.shape[0]
+    subs = big_ref.shape[1] // SUB
     planes = size // 4
     me = lax.axis_index("fsdp")
     tp = lax.axis_index("tp")
     z, x, core = me // 4, lax.rem(me // 2, 2), lax.rem(me, 2)
     heads_width = wqkv_ref.shape[2]
-    greet_group(size)
     partner = {"tp": 1 - tp}
 
     def to_core(plane, line):
@@ -361,151 +364,155 @@
             {"fsdp": me + 1 - 2 * core},
         )
 
-    def to_side(plane):
+    def band(sub):
+        return pl.ds(pl.multiple_of(sub * SUB, SUB), SUB)
+
+    def to_side(plane, sub):
+        slot = plane * subs + sub
         return send_to(
-            sum_ref.at[plane],
-            side_ref.at[plane],
-            x_send.at[plane],
-            x_recv.at[plane],
+            sum_ref.at[plane, band(sub)],
+            side_ref.at[plane, band(sub)],
+            x_send.at[slot],
+            x_recv.at[slot],
             {"fsdp": z * 4 + (1 - x) * 2 + core},
         )
 
-    def to_up(plane):
+    def to_up(plane, sub):
+        slot = plane * subs + sub
         return send_to(
-            usend_ref.at[plane],
-            urecv_ref.at[plane],
-            up_send.at[plane],
-            up_recv.at[plane],
+            usend_ref.at[plane, band(sub)],
+            urecv_ref.at[plane, band(sub)],
+            up_send.at[slot],
+            up_recv.at[slot],
             {"fsdp": lax.min(z + 1, planes - 1) * 4 + x * 2 + core},
         )
 
-    def to_down(plane):
+    def to_down(plane, sub):
+        slot = plane * subs + sub
         return send_to(
-            dsend_ref.at[plane],
-            drecv_ref.at[plane],
-            dn_send.at[plane],
-            dn_recv.at[plane],
+            dsend_ref.at[plane, band(sub)],
+            drecv_ref.at[plane, band(sub)],
+            dn_send.at[slot],
+            dn_recv.at[slot],
             {"fsdp": lax.max(z - 1, 0) * 4 + x * 2 + core},
         )
 
     lower = z < planes // 2
     order = [jnp.where(lower, planes - 1 - step, step) for step in range(planes)]
-    for plane in order:
-        to_core(plane, 1 - x).start()
-    for plane in order:
-        to_core(plane, x).start()
     out_y = send_to(other_ref, y_ref, y_send.at[0], y_recv.at[0], partner)
-    out_y.start()
-
     def joined(plane, line):
         to_core(plane, line).wait_recv()
         return wide(big_ref[plane * 4 + line * 2 + core]) + wide(core_ref[plane * 2 + line])
 
-    for plane in order:
-        sum_ref[plane] = low(joined(plane, 1 - x))
-        to_side(plane).start()
-    for plane in order:
-        acc_ref[plane] = joined(plane, x)
-
-    def rise(plane):
+    def rise(plane, sub):
         @pl.when(z < plane)
         def _():
             @pl.when(z > 0)
             def _():
-                to_up(plane).wait_recv()
-                acc_ref[plane] += wide(urecv_ref[plane])
-
-            usend_ref[plane] = low(acc_ref[plane])
-            to_up(plane).start()
-
-    def fall(plane):
+                to_up(plane, sub).wait_recv()
+                acc_ref[plane, band(sub)] += wide(urecv_ref[plane, band(sub)])
+
+            usend_ref[plane, band(sub)] = low(acc_ref[plane, band(sub)])
+            to_up(plane, sub).start()
+
+    def fall(plane, sub):
         @pl.when(z > plane)
         def _():
             @pl.when(z < planes - 1)
             def _():
-                to_down(plane).wait_recv()
-                acc_ref[plane] += wide(drecv_ref[plane])
-
-            dsend_ref[plane] = low(acc_ref[plane])
-            to_down(plane).start()
-
-    for step, plane in enumerate(order):
-        to_side(plane).wait_recv()
-        acc_ref[plane] += wide(side_ref[plane])
-        last_step = step == planes - 1
-
-        @pl.when(lower)
+                to_down(plane, sub).wait_recv()
+                acc_ref[plane, band(sub)] += wide(drecv_ref[plane, band(sub)])
+
+            dsend_ref[plane, band(sub)] = low(acc_ref[plane, band(sub)])
+            to_down(plane, sub).start()
+
+    def begin():
+        for plane in order:
+            to_core(plane, 1 - x).start()
+        for plane in order:
+            to_core(plane, x).start()
+        out_y.start()
+
+        for plane in order:
+            sum_ref[plane] = low(joined(plane, 1 - x))
+            each(0, subs, lambda sub: to_side(plane, sub).start())
+        for plane in order:
+            acc_ref[plane] = joined(plane, x)
+
+    def end():
+        for step, plane in enumerate(order):
+            last_step = step == planes - 1
+
+            def advance(sub):
+                to_side(plane, sub).wait_recv()
+                acc_ref[plane, band(sub)] += wide(side_ref[plane, band(sub)])
+
+                @pl.when(lower)
+                def _():
+                    (fall if last_step else rise)(plane, sub)
+
+                @pl.when(jnp.logical_not(lower))
+                def _():
+                    (rise if last_step else fall)(plane, sub)
+
+            each(0, subs, advance)
+
+        @pl.when(z > 0)
         def _():
-            (fall if last_step else rise)(plane)
-
-        @pl.when(jnp.logical_not(lower))
+            each(0, subs, lambda sub: to_up(z, sub).wait_recv())
+            acc_ref[z] += wide(urecv_ref[z])
+
+        @pl.when(z < planes - 1)
         def _():
-            (rise if last_step else fall)(plane)
-
-    @pl.when(z > 0)
-    def _():
-        to_up(z).wait_recv()
-        acc_ref[z] += wide(urecv_ref[z])
-
-    @pl.when(z < planes - 1)
-    def _():
-        to_down(z).wait_recv()
-        acc_ref[z] += wide(drecv_ref[z])
-
-    values = acc_ref[z]
-    red_ref[...] = values[:, : 4 * heads_width]
-    share = sum(
-        jnp.sum(
-            values[:, part * heads_width : (part + 1) * heads_width] * wide(wqkv_ref[part]),
-            axis=1,
-            keepdims=True,
-        )
-        for part in range(3)
-    )
-    last = values[:, 4 * heads_width :]
-    last = jnp.where(lax.broadcasted_iota(jnp.int32, last.shape, 1) == 0, share, last)
-    part_rows = tail_ref.shape[0]
-    tsend_ref[0] = last[:part_rows, :]
-    tsend_ref[1] = last[part_rows:, :]
-    tail_y = send_to(tsend_ref.at[1 - tp], trecv_ref, y_send.at[1], y_recv.at[1], partner)
-    tail_y.start()
-    out_y.wait()
-    tail_y.wait()
-    tail_ref[...] = tsend_ref[tp] + trecv_ref[...]
-    for plane in range(planes):
-        to_core(plane, 1 - x).wait_send()
-        to_core(plane, x).wait_send()
-        to_side(plane).wait_send()
-
-        @pl.when(z < plane)
-        def _():
-            to_up(plane).wait_send()
-
-        @pl.when(z > plane)
-        def _():
-            to_down(plane).wait_send()
-
-
-def run_finish(big, wqkv, other):
-    size = lax.axis_size("fsdp")
-    planes = size // 4
-    own_rows, width = other.shape
-    columns = big.shape[1]
-    shard = width // size
-    vmem = pl.BlockSpec(memory_space=pltpu.VMEM)
+            each(0, subs, lambda sub: to_down(z, sub).wait_recv())
+            acc_ref[z] += wide(drecv_ref[z])
+
+        values = acc_ref[z]
+        red_ref[...] = values[:, : 4 * heads_width]
+        share = sum(
+            jnp.sum(
+                values[:, part * heads_width : (part + 1) * heads_width] * wide(wqkv_ref[part]),
+                axis=1,
+                keepdims=True,
+            )
+            for part in range(3)
+        )
+        last = values[:, 4 * heads_width :]
+        last = jnp.where(lax.broadcasted_iota(jnp.int32, last.shape, 1) == 0, share, last)
+        part_rows = tail_ref.shape[0]
+        tsend_ref[0] = last[:part_rows, :]
+        tsend_ref[1] = last[part_rows:, :]
+        tail_y = send_to(tsend_ref.at[1 - tp], trecv_ref, y_send.at[1], y_recv.at[1], partner)
+        tail_y.start()
+        out_y.wait()
+        tail_y.wait()
+        tail_ref[...] = tsend_ref[tp] + trecv_ref[...]
+        for plane in range(planes):
+            to_core(plane, 1 - x).wait_send()
+            to_core(plane, x).wait_send()
+
+            def drain(sub):
+                to_side(plane, sub).wait_send()
+
+                @pl.when(z < plane)
+                def _():
+                    to_up(plane, sub).wait_send()
+
+                @pl.when(z > plane)
+                def _():
+                    to_down(plane, sub).wait_send()
+
+            each(0, subs, drain)
+
+    return begin, end
+
+
+def sum_scratch(planes, shard, columns):
     low_t, wide_t = jnp.bfloat16, jnp.float32
     dma = pltpu.SemaphoreType.DMA
     line = (planes, shard, columns)
-    return pl.pallas_call(
-        finish_kernel,
-        in_specs=[vmem] * 3,
-        out_specs=[vmem] * 3,
-        out_shape=[
-            jax.ShapeDtypeStruct((own_rows, width), low_t),
-            jax.ShapeDtypeStruct((shard, columns - PAIR), wide_t),
-            jax.ShapeDtypeStruct((shard // 2, PAIR), wide_t),
-        ],
-        scratch_shapes=[
+    return (
+        [
             pltpu.VMEM(line, low_t),
             pltpu.VMEM((2 * planes, shard, columns), low_t),
             pltpu.VMEM(line, low_t),
@@ -519,12 +526,9 @@
             dma((2 * planes,)),
             dma((2 * planes,)),
         ]
-        + [dma((planes,))] * 6
-        + [dma((2,))] * 2,
-        compiler_params=pltpu.CompilerParams(
-            collective_id=4, has_side_effects=True, vmem_limit_bytes=60 << 20
-        ),
-    )(big.reshape(size, shard, columns), wqkv, other)
+        + [dma((planes * (shard // SUB),))] * 6
+        + [dma((2,))] * 2
+    )
 
 
 def write_kernel(
@@ -550,10 +554,14 @@
     heads_width = attn_ref.shape[1]
     out_ref[...] = low(base_ref[...] + wide(y_ref[...]))
     hidden_ref[...] = grad_ref[...]
-    values = wide(expert_ref[0])
-    in_ref[0, :, 0, :] = values[:, :hidden]
-    in_ref[0, :, 1, :] = values[:, hidden : 2 * hidden]
-    down_ref[0] = values[:, 2 * hidden :]
+
+    def lay_out(e):
+        values = wide(expert_ref[e])
+        in_ref[e, :, 0, :] = values[:, :hidden]
+        in_ref[e, :, 1, :] = values[:, hidden : 2 * hidden]
+        down_ref[e] = values[:, 2 * hidden :]
+
+    each(0, expert_ref.shape[0], lay_out)
 
     @pl.when(pl.program_id(0) == 0)
     def _():
@@ -578,14 +586,15 @@
     experts, _, total = arrived.shape
     hidden = total // 3
     wide_t = jnp.float32
-    rows = pl.BlockSpec((own_rows // experts, width), lambda e: (e, 0))
+    steps = experts // 2
+    rows = pl.BlockSpec((own_rows // steps, width), lambda e: (e, 0))
 
     def whole(shape):
         return pl.BlockSpec(shape, lambda e: (0,) * len(shape))
 
     return pl.pallas_call(
         write_kernel,
-        grid=(experts,),
+        grid=(steps,),
         in_specs=[
             rows,
             rows,
@@ -593,7 +602,7 @@
             whole(red.shape),
             whole(tail.shape),
             whole(gains.shape),
-            pl.BlockSpec((1, shard, total), lambda e: (e, 0, 0)),
+            pl.BlockSpec((2, shard, total), lambda e: (e, 0, 0)),
         ],
         out_specs=[
             rows,
@@ -604,8 +613,8 @@
             whole((MIXING - ROUTER, count)),
             whole((VALUE - MIXING, count)),
             whole((2, count)),
-            pl.BlockSpec((1, shard, 2, hidden), lambda e: (e, 0, 0, 0)),
-            pl.BlockSpec((1, shard, hidden), lambda e: (e, 0, 0)),
+            pl.BlockSpec((2, shard, 2, hidden), lambda e: (e, 0, 0, 0)),
+            pl.BlockSpec((2, shard, hidden), lambda e: (e, 0, 0)),
         ],
         out_shape=[
             jax.ShapeDtypeStruct((own_rows, width), jnp.bfloat16),
@@ -1210,6 +1219,7 @@
     greet_group(size)
     partner = {"tp": 1 - tp}
     mine = pl.ds(pl.multiple_of(tp * own_rows, own_rows), own_rows)
+    hid_y = send_to(hid_own_ref, hid_ref.at[mine], y_send.at[1], y_recv.at[1], partner)
     stage_ref[...] = jnp.zeros_like(stage_ref)
     stage_ref[0:2, :small_rows] = gain_ref[...]
     stage_ref[ROUTER:MIXING, :small_rows] = wide(router_ref[...])
@@ -1220,12 +1230,20 @@
         small_all_ref.at[me, tp], small_all_ref.at[me, tp], y_send.at[0], y_recv.at[0], partner
     )
     small_y.start()
+    hid_y.start()
     for part in range(3):
         all_ref[me, :, part * heads_width : (part + 1) * heads_width] = wqkv_ref[part]
     all_ref[me, :, 3 * heads_width :] = wout_ref[...]
-    hid_y = send_to(hid_own_ref, hid_ref.at[mine], y_send.at[1], y_recv.at[1], partner)
     tok_y = send_to(tok_all_ref.at[tp], tok_all_ref.at[tp], y_send.at[2], y_recv.at[2], partner)
-    cot_y = send_to(cot_own_ref, cot_ref.at[mine], y_send.at[3], y_recv.at[3], partner)
+
+    def cot_copy(part):
+        count = own_rows // 4
+        near = pl.ds(part * count, count)
+        far = pl.ds(pl.multiple_of(tp * own_rows + part * count, count), count)
+        return send_to(
+            cot_own_ref.at[near], cot_ref.at[far], y_send.at[3 + part], y_recv.at[3 + part], partner
+        )
+
     experts = CoreExchange(shard_ref, expert_ref, wsend_sem, wrecv_sem)
     expert_count, _, hidden = wdown_ref.shape
 
@@ -1294,10 +1312,10 @@
         sibling(kind, z, x, core).start()
 
     launch(0)
-    hid_y.start()
     stage_tokens()
     tok_y.start()
-    cot_y.start()
+    for part in range(4):
+        cot_copy(part).start()
     hid_ref[mine, :] = hid_own_ref[...]
     cot_ref[mine, :] = cot_own_ref[...]
     small_y.wait()
@@ -1383,7 +1401,8 @@
     def between():
         for store in stores[1:4]:
             store.start()
-        cot_y.wait()
+        for part in range(4):
+            cot_copy(part).wait()
         stores[4].start()
 
     attend(
@@ -1428,7 +1447,9 @@
     experts.wait()
 
 
-def backward_kernel(
+def backward_body(
+    begin,
+    end,
     res_ref,
     dx_ref,
     slot_ref,
@@ -1612,11 +1633,12 @@
             columns.append((MIXING + 2 * c + 1, -slope))
             value_columns.append((VALUE + c, weight * a1))
         value_matrix = lane_matrix(tok.shape, value_columns)
-        base = mid + alpha * normed + nt_dot(low(value_matrix), small)
 
         @pl.when(mine)
         def _():
-            base_ref[slab_of(block), :] += base
+            base_ref[slab_of(block), :] += (
+                mid + alpha * normed + nt_dot(low(value_matrix), small)
+            )
 
         row_copy(block).wait()
         share_copy(block).wait()
@@ -1708,16 +1730,21 @@
     s1_turned = s1_ref[...].T
     for part in range(3):
         lanes = slice(part * heads_width, (part + 1) * heads_width)
-        big_ref[:, lanes] = low(nn_dot(s1_turned, gp_ref[:, lanes]))
-    big_ref[:, 3 * heads_width : 4 * heads_width] = low(tn_dot(att_ref[...], mixed_ref[...]))
+        big_ref[:, :, lanes] = low(nn_dot(s1_turned, gp_ref[:, lanes])).reshape(
+            big_ref.shape[:2] + (heads_width,)
+        )
+    big_ref[:, :, 3 * heads_width : 4 * heads_width] = low(
+        tn_dot(att_ref[...], mixed_ref[...])
+    ).reshape(big_ref.shape[:2] + (heads_width,))
     tall = jnp.where(
         lax.broadcasted_iota(jnp.int32, (PAIR, width), 0) == 1,
         jnp.broadcast_to(acc_gain_ref[0:1, :], (PAIR, width)),
         0.0,
     )
-    big_ref[:, 4 * heads_width :] = low(
+    big_ref[:, :, 4 * heads_width :] = low(
         tn_dot(s2_ref[...], slope_ref[...]) + tn_dot(cot_ref[...], value_ref[...]) + tall.T
-    )
+    ).reshape(big_ref.shape[:2] + (PAIR,))
+    begin()
     for slot in reversed(range(half_blocks)):
         slab = slice(slot * BLOCK, (slot + 1) * BLOCK)
         stream_copy(slot).wait()
@@ -1729,7 +1756,23 @@
         grad_ref[slab, :] = gmid_ref[mid_rows, :] + scale * (
             scaled - unit * mean_last(scaled * unit)
         )
+    end()
     experts.wait()
+
+
+def backward_plain_kernel(*refs):
+    backward_body(lambda: None, lambda: None, *refs)
+
+
+def backward_kernel(body_count, *refs):
+    operands, wqkv_ref = refs[:16], refs[16]
+    grad_ref, base_ref, arrived_ref, y_ref, red_ref, tail_ref = refs[17:23]
+    other_ref, big_ref = refs[23:25]
+    body, sums = refs[25 : 25 + body_count], refs[25 + body_count :]
+    begin, end = sum_stages(big_ref, wqkv_ref, other_ref, y_ref, red_ref, tail_ref, *sums)
+    backward_body(
+        begin, end, *operands, grad_ref, base_ref, other_ref, big_ref, arrived_ref, *body
+    )
 
 
 def forward_results(length, width, heads_width, shard):
@@ -1818,8 +1861,8 @@
             dma((count,)),
             dma((experts,)),
             dma((experts,)),
-            dma((4,)),
-            dma((4,)),
+            dma((7,)),
+            dma((7,)),
         ]
         + [dma((2, size // 4))] * 6
         + [dma((2, size // 2))] * 2
@@ -1830,7 +1873,7 @@
     )(*operands)
 
 
-def run_backward(*operands):
+def run_backward(wqkv, *operands):
     cot, mid, s1, qkv, mixed, blocks, own, egrads = (
         operands[index] for index in (4, 5, 6, 7, 9, 10, 14, 15)
     )
@@ -1838,64 +1881,88 @@
     heads_width = mixed.shape[1]
     count = length // BLOCK
     own_rows = own.shape[0]
+    parts, shard = blocks.shape[:2]
+    columns = 4 * heads_width + PAIR
     vmem = pl.BlockSpec(memory_space=pltpu.VMEM)
     hbm = pl.BlockSpec(memory_space=pl.ANY)
     low_t, wide_t = jnp.bfloat16, jnp.float32
     dma = pltpu.SemaphoreType.DMA
+    in_specs = [vmem] * 5 + [hbm] * 3 + [vmem] + [hbm] * 2 + [vmem] * 4 + [hbm]
+    body = [
+        pltpu.VMEM((count, BLOCK, width), low_t),
+        pltpu.VMEM((count, BLOCK, width), low_t),
+        pltpu.VMEM((count, 8, BLOCK), wide_t),
+        pltpu.VMEM((count, 8, BLOCK), wide_t),
+        pltpu.VMEM(mid.shape, wide_t),
+        pltpu.VMEM(s1.shape, low_t),
+        pltpu.VMEM(qkv.shape, low_t),
+        pltpu.VMEM(mixed.shape, low_t),
+        pltpu.VMEM(blocks.shape, low_t),
+        pltpu.VMEM((2, BLOCK, width), low_t),
+        pltpu.VMEM((2, BLOCK, width), low_t),
+        pltpu.VMEM((length, width), wide_t),
+        pltpu.VMEM((2, BLOCK, width), wide_t),
+        pltpu.VMEM((heads_width, length), low_t),
+        pltpu.VMEM((BLOCK, heads_width), low_t),
+        pltpu.VMEM((length, heads_width), wide_t),
+        pltpu.VMEM((length, heads_width), wide_t),
+        pltpu.VMEM((length, 3 * heads_width), low_t),
+        pltpu.VMEM((length, width), low_t),
+        pltpu.VMEM((length, width), low_t),
+        pltpu.VMEM((length, PAIR), low_t),
+        pltpu.VMEM((length, PAIR), low_t),
+        pltpu.VMEM((8, width), wide_t),
+        dma((count,)),
+        dma((count,)),
+        dma((2,)),
+        dma((2,)),
+        dma((egrads.shape[0],)),
+        dma((egrads.shape[0],)),
+        dma((count,)),
+        dma((count,)),
+        dma((5,)),
+    ]
+    own_wide = jax.ShapeDtypeStruct((own_rows, width), wide_t)
+    own_low = jax.ShapeDtypeStruct((own_rows, width), low_t)
+    arrived = jax.ShapeDtypeStruct(egrads.shape, low_t)
+    params = pltpu.CompilerParams(
+        collective_id=1, has_side_effects=True, vmem_limit_bytes=67043328
+    )
+    if wqkv is None:
+        return pl.pallas_call(
+            backward_plain_kernel,
+            in_specs=in_specs,
+            out_specs=[vmem] * 4 + [hbm],
+            out_shape=[
+                own_wide,
+                own_wide,
+                own_low,
+                jax.ShapeDtypeStruct((parts, shard, columns), low_t),
+                arrived,
+            ],
+            scratch_shapes=body,
+            compiler_params=params,
+        )(*operands)
     return pl.pallas_call(
-        backward_kernel,
-        in_specs=[vmem] * 5
-        + [hbm] * 3
-        + [vmem]
-        + [hbm] * 2
-        + [vmem] * 4
-        + [hbm],
-        out_specs=[vmem] * 4 + [hbm],
+        functools.partial(backward_kernel, len(body)),
+        in_specs=in_specs + [vmem],
+        out_specs=[vmem] * 2 + [hbm] + [vmem] * 3,
         out_shape=[
-            jax.ShapeDtypeStruct((own_rows, width), wide_t),
-            jax.ShapeDtypeStruct((own_rows, width), wide_t),
-            jax.ShapeDtypeStruct((own_rows, width), low_t),
-            jax.ShapeDtypeStruct((width, 4 * heads_width + PAIR), low_t),
-            jax.ShapeDtypeStruct(egrads.shape, low_t),
+            own_wide,
+            own_wide,
+            arrived,
+            own_low,
+            jax.ShapeDtypeStruct((shard, columns - PAIR), wide_t),
+            jax.ShapeDtypeStruct((shard // 2, PAIR), wide_t),
         ],
         scratch_shapes=[
-            pltpu.VMEM((count, BLOCK, width), low_t),
-            pltpu.VMEM((count, BLOCK, width), low_t),
-            pltpu.VMEM((count, 8, BLOCK), wide_t),
-            pltpu.VMEM((count, 8, BLOCK), wide_t),
-            pltpu.VMEM(mid.shape, wide_t),
-            pltpu.VMEM(s1.shape, low_t),
-            pltpu.VMEM(qkv.shape, low_t),
-            pltpu.VMEM(mixed.shape, low_t),
-            pltpu.VMEM(blocks.shape, low_t),
-            pltpu.VMEM((2, BLOCK, width), low_t),
-            pltpu.VMEM((2, BLOCK, width), low_t),
-            pltpu.VMEM((length, width), wide_t),
-            pltpu.VMEM((2, BLOCK, width), wide_t),
-            pltpu.VMEM((heads_width, length), low_t),
-            pltpu.VMEM((BLOCK, heads_width), low_t),
-            pltpu.VMEM((length, heads_width), wide_t),
-            pltpu.VMEM((length, heads_width), wide_t),
-            pltpu.VMEM((length, 3 * heads_width), low_t),
-            pltpu.VMEM((length, width), low_t),
-            pltpu.VMEM((length, width), low_t),
-            pltpu.VMEM((length, PAIR), low_t),
-            pltpu.VMEM((length, PAIR), low_t),
-            pltpu.VMEM((8, width), wide_t),
-            dma((count,)),
-            dma((count,)),
-            dma((2,)),
-            dma((2,)),
-            dma((egrads.shape[0],)),
-            dma((egrads.shape[0],)),
-            dma((count,)),
-            dma((count,)),
-            dma((5,)),
-        ],
-        compiler_params=pltpu.CompilerParams(
-            collective_id=1, has_side_effects=True, vmem_limit_bytes=60 << 20
-        ),
-    )(*operands)
+            pltpu.VMEM((own_rows, width), low_t),
+            pltpu.VMEM((parts, shard, columns), low_t),
+        ]
+        + body
+        + sum_scratch(parts // 4, shard, columns),
+        compiler_params=params,
+    )(*operands, wqkv)
 
 
 def shards(
@@ -1960,7 +2027,8 @@
     results, grad_rows, grads_exp = run_expert(
         s2, cot, lines, jnp.broadcast_to(slot[:, None], (slot.shape[0], PAIR)), expert_weights
     )
-    grad_hidden, base, for_other, big, arrived = run_backward(
+    backward = run_backward(
+        wqkv if planned else None,
         results.reshape(-1, width),
         grad_rows.reshape(-1, width),
         jnp.broadcast_to(slot[None, :], (8, slot.shape[0])),
@@ -1978,7 +2046,11 @@
         hidden,
         split_grads(grads_exp),
     )
-    received, red, last = (run_finish if planned else finish_plain)(big, wqkv, for_other)
+    if planned:
+        grad_hidden, base, arrived, received, red, last = backward
+    else:
+        grad_hidden, base, for_other, big, arrived = backward
+        received, red, last = finish_plain(big.reshape(width, -1), wqkv, for_other)
     output, grad_hidden, grad_qkv, grad_attn_out, gain_grads, grad_router, grad_mixing, grad_value, grad_in, grad_out = run_write(
         base, received, grad_hidden, red, last, gains, arrived
     )

time: 322 us -> 309 us (0.960)
  Pallas kernels: 313 us -> 301 us
    pallas_call x3 -> x2, Pallas kernels: 98.8 us -> 86.4 us  [the longest x1 79.7 us: run_backward(): pl.pallas_call(functools.partial(backward_kernel, len(body)), in_specs=in...]
where the time goes in v1:
time: 309 us; the launch traced here: 306 us
  Pallas kernels  301 us (97%)
    pallas_call x1, Pallas kernels, run_expert(): pl.pallas_call(expert_kernel, in_specs=[vmem] * 4 + [pl.BlockSpec(memory_...  134 us
    pallas_call x1, Pallas kernels, run_forward(): pl.pallas_call(forward_kernel, in_specs=[vmem] * 15, out_specs=[hbm, vmem...  80.7 us
    pallas_call x1, Pallas kernels, run_backward(): pl.pallas_call(functools.partial(backward_kernel, len(body)), in_specs=in...  79.7 us
    pallas_call x1, Pallas kernels, run_write(): pl.pallas_call(write_kernel, grid=(steps,), in_specs=[rows, rows, rows, w...  6.65 us

profile of v1, /device:TPU:12, one launch (start us, length us, event | category | flops | bytes accessed | tf_op | source)
XLA Modules:
  0.0 305.7 jit_solution(3359613680441896402)
XLA Ops:
  0.7 1.3 maximum_convert_fusion.gain_ref
  2.0 0.6 broadcast_in_dim.5.refs_2_
  2.6 0.9 broadcast_in_dim.4.slot_ref
  3.5 80.7 %shard_map.239 = (bf16[16,48,1536]{2,1,0:T(8,128)(2,1)}, bf16[768,128]{1,0:T(8,128)(2,1)}, f32[8,768]{1,0:T(8,128)}, bf16[1024,768]{1,0:T(8,128)(2,1)}, bf16[102...) custom-call(bf16[512,768]{1,0:T(8,128)(2,1)} %refs_14_.1, ...), custom_call_target="tpu_custom_call" | custom-call | tf_op jit(solution)/shard_map/pallas_call | solution.py:1834
  84.2 133.8 %shard_map.240 = (bf16[16,48,768]{2,1,0:T(8,128)(2,1)}, bf16[16,48,768]{2,1,0:T(8,128)(2,1)}, bf16[8,48,3072]{2,1,0:T(8,128)(2,1)}) custom-call(bf16[1024,768]{1,0:T(8,128)(2,1)} %get-tuple-element.43.s2_ref, bf16[1024,768]{1,0:T(8,128)(2,1)} %get-tuple-element.44.cot_ref.refs_4_, f32[8,1024]{1,0:T(8,128)} %get-tuple-element.45.line_ref, ...), custom_call_target="tpu_custom_call" | custom-call | tf_op jit(solution)/shard_map/pallas_call | solution.py:933
  218.1 79.7 %shard_map.241 = (f32[512,768]{1,0:T(8,128)}, f32[512,768]{1,0:T(8,128)}, bf16[8,48,3072]{2,1,0:T(8,128)(2,1)}, bf16[512,768]{1,0:T(8,128)(2,1)}, f32[48,1536]{1,0:T(8,128)}, /*index=5*/f32[24,128]{1,0:T(8,128)}) custom-call(bf16[768,768]{1,0:T(8,128)(2,1)} %bitcast.20, bf16[768,768]{1,0:T(8,128)(2,1)} %bitcast.21, f32[8,768]{1,0:T(8,128)} %broadcast_in_dim.5.refs_2_, ...), custom_call_target="tpu_custom_call" | custom-call | tf_op jit(solution)/shard_map/pallas_call | solution.py:1946
  297.8 6.6 %shard_map.242 = (bf16[512,768]{1,0:T(8,128)(2,1)}, f32[512,768]{1,0:T(8,128)}, f32[3,48,384]{2,1,0:T(8,128)}, f32[48,384]{1,0:T(8,128)}, f32[2,24]{1,0:T(2,128)...) custom-call(f32[512,768]{1,0:T(8,128)} %get-tuple-element.59.base_re, ...), custom_call_target="tpu_custom_call" | custom-call | tf_op jit(solution)/shard_map/pallas_call | solution.py:595
  304.4 1.3 slice_bitcast_fusion
  (1 shorter events, 0.0 us)

commit v2 on v1

--- a/solution.py
+++ b/solution.py
@@ -305,11 +305,10 @@
         self.experts, self.copy, self.arrival = experts, copy, arrival
         self.local = pltpu.make_async_copy(source.at[mine], target.at[mine], send_sem.at[0])
 
-    def start(self, done=()):
+    def start(self, order=(1, 2, 3, 4, 5, 6, 7)):
         self.local.start()
-        for k in range(1, self.experts):
-            if k not in done:
-                self.copy(k).start()
+        for k in order:
+            self.copy(k).start()
 
     def wait(self):
         each(1, self.experts, lambda k: self.copy(k).wait_send())
@@ -399,7 +398,14 @@
 
     lower = z < planes // 2
     order = [jnp.where(lower, planes - 1 - step, step) for step in range(planes)]
-    out_y = send_to(other_ref, y_ref, y_send.at[0], y_recv.at[0], partner)
+    half_rows = other_ref.shape[0] // 2
+
+    def out_y(part):
+        rows = pl.ds(part * half_rows, half_rows)
+        return send_to(
+            other_ref.at[rows], y_ref.at[rows], y_send.at[2 * part], y_recv.at[2 * part], partner
+        )
+
     def joined(plane, line):
         to_core(plane, line).wait_recv()
         return wide(big_ref[plane * 4 + line * 2 + core]) + wide(core_ref[plane * 2 + line])
@@ -431,7 +437,7 @@
             to_core(plane, 1 - x).start()
         for plane in order:
             to_core(plane, x).start()
-        out_y.start()
+        out_y(1).start()
 
         for plane in order:
             sum_ref[plane] = low(joined(plane, 1 - x))
@@ -439,7 +445,7 @@
         for plane in order:
             acc_ref[plane] = joined(plane, x)
 
-    def end():
+    def middle():
         for step, plane in enumerate(order):
             last_step = step == planes - 1
 
@@ -457,6 +463,7 @@
 
             each(0, subs, advance)
 
+    def end():
         @pl.when(z > 0)
         def _():
             each(0, subs, lambda sub: to_up(z, sub).wait_recv())
@@ -484,7 +491,8 @@
         tsend_ref[1] = last[part_rows:, :]
         tail_y = send_to(tsend_ref.at[1 - tp], trecv_ref, y_send.at[1], y_recv.at[1], partner)
         tail_y.start()
-        out_y.wait()
+        out_y(0).wait()
+        out_y(1).wait()
         tail_y.wait()
         tail_ref[...] = tsend_ref[tp] + trecv_ref[...]
         for plane in range(planes):
@@ -504,7 +512,7 @@
 
             each(0, subs, drain)
 
-    return begin, end
+    return lambda: out_y(0).start(), begin, middle, end
 
 
 def sum_scratch(planes, shard, columns):
@@ -527,7 +535,7 @@
             dma((2 * planes,)),
         ]
         + [dma((planes * (shard // SUB),))] * 6
-        + [dma((2,))] * 2
+        + [dma((3,))] * 2
     )
 
 
@@ -1004,7 +1012,7 @@
         rows = block_rows(block)
         source = wide(hid_ref[rows, :])
         s1 = low(source * lax.rsqrt(mean_last(source * source) + EPSILON) * gain_one)
-        s1_ref[rows, :] = s1
+        s1_ref[:, rows] = s1.T
         cosine, sine = spread_table(table_ref, block)
         for part in range(3):
             projected = nn_dot(s1, weight(part))
@@ -1448,8 +1456,7 @@
 
 
 def backward_body(
-    begin,
-    end,
+    stages,
     res_ref,
     dx_ref,
     slot_ref,
@@ -1563,7 +1570,8 @@
         onehots = [low(jnp.where(column(tok, TARGET + m) == slot_row, 1.0, 0.0)) for m in range(2)]
         gsend_ref[block] = low(nn_dot(onehots[0] + onehots[1], dx_ref[...]))
         row_copy(block).start()
-        placed = [nn_dot(onehot, res_ref[...]) for onehot in onehots]
+        both = nn_dot(jnp.concatenate(onehots, axis=0), res_ref[...])
+        placed = [both[:BLOCK], both[BLOCK:]]
         cot_wide = wide(cot_ref[rows, :])
         shares = [
             column(tok, GATE + m) * jnp.sum(placed[m] * cot_wide, axis=1, keepdims=True)
@@ -1581,7 +1589,9 @@
         def _():
             other_ref[slab_of(block), :] = low(mixture)
 
+    early, begin, middle, end = stages
     backwards(send_rows)
+    early()
     for load in loads:
         load.wait()
     kt_ref[...] = qkv_ref[:, heads_width : 2 * heads_width].T
@@ -1727,10 +1737,9 @@
             stream_copy(slot).start()
 
     backwards(main)
-    s1_turned = s1_ref[...].T
     for part in range(3):
         lanes = slice(part * heads_width, (part + 1) * heads_width)
-        big_ref[:, :, lanes] = low(nn_dot(s1_turned, gp_ref[:, lanes])).reshape(
+        big_ref[:, :, lanes] = low(nn_dot(s1_ref[...], gp_ref[:, lanes])).reshape(
             big_ref.shape[:2] + (heads_width,)
         )
     big_ref[:, :, 3 * heads_width : 4 * heads_width] = low(
@@ -1745,6 +1754,7 @@
         tn_dot(s2_ref[...], slope_ref[...]) + tn_dot(cot_ref[...], value_ref[...]) + tall.T
     ).reshape(big_ref.shape[:2] + (PAIR,))
     begin()
+    middle()
     for slot in reversed(range(half_blocks)):
         slab = slice(slot * BLOCK, (slot + 1) * BLOCK)
         stream_copy(slot).wait()
@@ -1761,7 +1771,7 @@
 
 
 def backward_plain_kernel(*refs):
-    backward_body(lambda: None, lambda: None, *refs)
+    backward_body([lambda: None] * 4, *refs)
 
 
 def backward_kernel(body_count, *refs):
@@ -1769,16 +1779,14 @@
     grad_ref, base_ref, arrived_ref, y_ref, red_ref, tail_ref = refs[17:23]
     other_ref, big_ref = refs[23:25]
     body, sums = refs[25 : 25 + body_count], refs[25 + body_count :]
-    begin, end = sum_stages(big_ref, wqkv_ref, other_ref, y_ref, red_ref, tail_ref, *sums)
-    backward_body(
-        begin, end, *operands, grad_ref, base_ref, other_ref, big_ref, arrived_ref, *body
-    )
+    stages = sum_stages(big_ref, wqkv_ref, other_ref, y_ref, red_ref, tail_ref, *sums)
+    backward_body(stages, *operands, grad_ref, base_ref, other_ref, big_ref, arrived_ref, *body)
 
 
 def forward_results(length, width, heads_width, shard):
     low_t, wide_t = jnp.bfloat16, jnp.float32
     return [
-        jax.ShapeDtypeStruct((length, width), low_t),
+        jax.ShapeDtypeStruct((width, length), low_t),
         jax.ShapeDtypeStruct((length, 3 * heads_width), low_t),
         jax.ShapeDtypeStruct((8, length), wide_t),
         jax.ShapeDtypeStruct((length, heads_width), low_t),
@@ -1845,7 +1853,7 @@
         + forward_results(length, width, heads_width, (experts, shard, 3 * hidden)),
         scratch_shapes=[
             pltpu.VMEM((size, shard, 4 * heads_width), low_t),
-            pltpu.VMEM((length, width), low_t),
+            pltpu.VMEM((width, length), low_t),
             pltpu.VMEM((length, 3 * heads_width), low_t),
             pltpu.VMEM((length, heads_width), low_t),
             pltpu.VMEM((length, width), low_t),

time: 309 us -> 309 us (level)
  no operation moved by 1% of the time
where the time goes in v2:
time: 309 us; the launch traced here: 304 us
  Pallas kernels  299 us (97%)
    pallas_call x1, Pallas kernels, run_expert(): pl.pallas_call(expert_kernel, in_specs=[vmem] * 4 + [pl.BlockSpec(memory_...  134 us
    pallas_call x1, Pallas kernels, run_forward(): pl.pallas_call(forward_kernel, in_specs=[vmem] * 15, out_specs=[hbm, vmem...  80.7 us
    pallas_call x1, Pallas kernels, run_backward(): pl.pallas_call(functools.partial(backward_kernel, len(body)), in_specs=in...  77.5 us
    pallas_call x1, Pallas kernels, run_write(): pl.pallas_call(write_kernel, grid=(steps,), in_specs=[rows, rows, rows, w...  6.65 us

profile of v2, /device:TPU:12, one launch (start us, length us, event | category | flops | bytes accessed | tf_op | source)
XLA Modules:
  0.0 303.6 jit_solution(16348292958498755622)
XLA Ops:
  0.7 1.3 maximum_convert_fusion.gain_ref
  2.0 0.6 broadcast_in_dim.5.refs_2_
  2.6 0.9 broadcast_in_dim.4.slot_ref
  3.5 80.7 %shard_map.239 = (bf16[16,48,1536]{2,1,0:T(8,128)(2,1)}, bf16[768,128]{1,0:T(8,128)(2,1)}, f32[8,768]{1,0:T(8,128)}, bf16[768,1024]{1,0:T(8,128)(2,1)}, bf16[102...) custom-call(bf16[512,768]{1,0:T(8,128)(2,1)} %refs_14_.1, ...), custom_call_target="tpu_custom_call" | custom-call | tf_op jit(solution)/shard_map/pallas_call | solution.py:1842
  84.2 134.0 %shard_map.240 = (bf16[16,48,768]{2,1,0:T(8,128)(2,1)}, bf16[16,48,768]{2,1,0:T(8,128)(2,1)}, bf16[8,48,3072]{2,1,0:T(8,128)(2,1)}) custom-call(bf16[1024,768]{1,0:T(8,128)(2,1)} %get-tuple-element.43.s2_ref, bf16[1024,768]{1,0:T(8,128)(2,1)} %get-tuple-element.44.cot_ref.refs_4_, f32[8,1024]{1,0:T(8,128)} %get-tuple-element.45.line_ref, ...), custom_call_target="tpu_custom_call" | custom-call | tf_op jit(solution)/shard_map/pallas_call | solution.py:941
  218.2 77.5 %shard_map.241 = (f32[512,768]{1,0:T(8,128)}, f32[512,768]{1,0:T(8,128)}, bf16[8,48,3072]{2,1,0:T(8,128)(2,1)}, bf16[512,768]{1,0:T(8,128)(2,1)}, f32[48,1536]{1,0:T(8,128)}, /*index=5*/f32[24,128]{1,0:T(8,128)}) custom-call(bf16[768,768]{1,0:T(8,128)(2,1)} %bitcast.20, bf16[768,768]{1,0:T(8,128)(2,1)} %bitcast.21, f32[8,768]{1,0:T(8,128)} %broadcast_in_dim.5.refs_2_, ...), custom_call_target="tpu_custom_call" | custom-call | tf_op jit(solution)/shard_map/pallas_call | solution.py:1954
  295.7 6.6 %shard_map.242 = (bf16[512,768]{1,0:T(8,128)(2,1)}, f32[512,768]{1,0:T(8,128)}, f32[3,48,384]{2,1,0:T(8,128)}, f32[48,384]{1,0:T(8,128)}, f32[2,24]{1,0:T(2,128)...) custom-call(f32[512,768]{1,0:T(8,128)} %get-tuple-element.59.base_re, ...), custom_call_target="tpu_custom_call" | custom-call | tf_op jit(solution)/shard_map/pallas_call | solution.py:603
  302.4 1.3 slice_bitcast_fusion
  (1 shorter events, 0.0 us)

commit v3 on v1

--- a/solution.py
+++ b/solution.py
@@ -633,7 +633,7 @@
 
 def expert_kernel(
     s2_ref,
-    cot_ref,
+    cot_hbm,
     line_ref,
     slot_ref,
     weight_ref,
@@ -671,7 +671,11 @@
     rr_sem,
     ds_sem,
     dr_sem,
+    cot_ref,
+    cot_sem,
 ):
+    cot_load = pltpu.make_async_copy(cot_hbm, cot_ref, cot_sem.at[0])
+    cot_load.start()
     peers, rows, width = xs_ref.shape
     total = peers * rows
     hidden = gate_ref.shape[1]
@@ -802,6 +806,7 @@
 
     each(0, 2, pack_x)
     there.start()
+    cot_load.wait()
     each(0, 2, pack_g)
 
     def forward_x(k):
@@ -932,7 +937,8 @@
     block = (peers, rows, width)
     return pl.pallas_call(
         expert_kernel,
-        in_specs=[vmem] * 4 + [pl.BlockSpec(memory_space=pl.ANY)],
+        in_specs=[vmem, pl.BlockSpec(memory_space=pl.ANY), vmem, vmem]
+        + [pl.BlockSpec(memory_space=pl.ANY)],
         out_specs=[vmem] * 3,
         out_shape=[
             jax.ShapeDtypeStruct(block, low_t),
@@ -960,7 +966,8 @@
         ]
         + [dma((peers,))] * 8
         + [dma((2, peers))] * 2
-        + [dma((peers,))] * 4,
+        + [dma((peers,))] * 4
+        + [pltpu.VMEM(cot.shape, low_t), dma((1,))],
         compiler_params=pltpu.CompilerParams(
             collective_id=2, has_side_effects=True, vmem_limit_bytes=67043328
         ),
@@ -1450,11 +1457,11 @@
 def backward_body(
     begin,
     end,
-    res_ref,
+    res_hbm,
     dx_ref,
     slot_ref,
     tok_ref,
-    cot_ref,
+    cot_hbm,
     mid_hbm,
     s1_hbm,
     qkv_hbm,
@@ -1503,7 +1510,16 @@
     ssend_sem,
     srecv_sem,
     load_sem,
+    res_ref,
+    cot_ref,
+    first_sem,
 ):
+    first = [
+        pltpu.make_async_copy(res_hbm, res_ref, first_sem.at[0]),
+        pltpu.make_async_copy(cot_hbm, cot_ref, first_sem.at[1]),
+    ]
+    for load in first:
+        load.start()
     loads = [
         pltpu.make_async_copy(source, target, load_sem.at[index])
         for index, (source, target) in enumerate(
@@ -1563,6 +1579,12 @@
         onehots = [low(jnp.where(column(tok, TARGET + m) == slot_row, 1.0, 0.0)) for m in range(2)]
         gsend_ref[block] = low(nn_dot(onehots[0] + onehots[1], dx_ref[...]))
         row_copy(block).start()
+
+        @pl.when(block == blocks - 1)
+        def _():
+            for load in first:
+                load.wait()
+
         placed = [nn_dot(onehot, res_ref[...]) for onehot in onehots]
         cot_wide = wide(cot_ref[rows, :])
         shares = [
@@ -1887,7 +1909,7 @@
     hbm = pl.BlockSpec(memory_space=pl.ANY)
     low_t, wide_t = jnp.bfloat16, jnp.float32
     dma = pltpu.SemaphoreType.DMA
-    in_specs = [vmem] * 5 + [hbm] * 3 + [vmem] + [hbm] * 2 + [vmem] * 4 + [hbm]
+    in_specs = [hbm] + [vmem] * 3 + [hbm] * 4 + [vmem] + [hbm] * 2 + [vmem] * 4 + [hbm]
     body = [
         pltpu.VMEM((count, BLOCK, width), low_t),
         pltpu.VMEM((count, BLOCK, width), low_t),
@@ -1921,6 +1943,9 @@
         dma((count,)),
         dma((count,)),
         dma((5,)),
+        pltpu.VMEM(operands[0].shape, low_t),
+        pltpu.VMEM(cot.shape, low_t),
+        dma((2,)),
     ]
     own_wide = jax.ShapeDtypeStruct((own_rows, width), wide_t)
     own_low = jax.ShapeDtypeStruct((own_rows, width), low_t)

time: 309 us -> 308 us (level)
  no operation moved by 1% of the time
where the time goes in v3:
time: 308 us; the launch traced here: 304 us
  Pallas kernels  300 us (97%)
    pallas_call x1, Pallas kernels, run_expert(): pl.pallas_call(expert_kernel, in_specs=[vmem, pl.BlockSpec(memory_space=p...  133 us
    pallas_call x1, Pallas kernels, run_forward(): pl.pallas_call(forward_kernel, in_specs=[vmem] * 15, out_specs=[hbm, vmem...  80.7 us
    pallas_call x1, Pallas kernels, run_backward(): pl.pallas_call(functools.partial(backward_kernel, len(body)), in_specs=in...  78.9 us
    pallas_call x1, Pallas kernels, run_write(): pl.pallas_call(write_kernel, grid=(steps,), in_specs=[rows, rows, rows, w...  6.65 us

profile of v3, /device:TPU:12, one launch (start us, length us, event | category | flops | bytes accessed | tf_op | source)
XLA Modules:
  0.0 304.4 jit_solution(13120175943314086611)
XLA Ops:
  0.7 1.3 maximum_convert_fusion.gain_ref
  2.0 0.6 broadcast_in_dim.5.refs_2_
  2.6 0.9 broadcast_in_dim.4.slot_ref
  3.5 80.7 %shard_map.239 = (bf16[16,48,1536]{2,1,0:T(8,128)(2,1)}, bf16[768,128]{1,0:T(8,128)(2,1)}, f32[8,768]{1,0:T(8,128)}, bf16[1024,768]{1,0:T(8,128)(2,1)}, bf16[102...) custom-call(bf16[512,768]{1,0:T(8,128)(2,1)} %refs_14_.1, ...), custom_call_target="tpu_custom_call" | custom-call | tf_op jit(solution)/shard_map/pallas_call | solution.py:1856
  84.2 133.4 %shard_map.240 = (bf16[16,48,768]{2,1,0:T(8,128)(2,1)}, bf16[16,48,768]{2,1,0:T(8,128)(2,1)}, bf16[8,48,3072]{2,1,0:T(8,128)(2,1)}) custom-call(bf16[1024,768]{1,0:T(8,128)(2,1)} %get-tuple-element.43.s2_ref, bf16[1024,768]{1,0:T(8,128)(2,1)} %get-tuple-element.44.cot_hbm.refs_4_, f32[8,1024]{1,0:T(8,128)} %get-tuple-element.45.line_ref, ...), custom_call_target="tpu_custom_call" | custom-call | tf_op jit(solution)/shard_map/pallas_call | solution.py:938
  217.6 78.9 %shard_map.241 = (f32[512,768]{1,0:T(8,128)}, f32[512,768]{1,0:T(8,128)}, bf16[8,48,3072]{2,1,0:T(8,128)(2,1)}, bf16[512,768]{1,0:T(8,128)(2,1)}, f32[48,1536]{1,0:T(8,128)}, /*index=5*/f32[24,128]{1,0:T(8,128)}) custom-call(bf16[768,768]{1,0:T(8,128)(2,1)} %bitcast.20, bf16[768,768]{1,0:T(8,128)(2,1)} %bitcast.21, f32[8,768]{1,0:T(8,128)} %broadcast_in_dim.5.refs_2_, ...), custom_call_target="tpu_custom_call" | custom-call | tf_op jit(solution)/shard_map/pallas_call | solution.py:1971
  296.5 6.6 %shard_map.242 = (bf16[512,768]{1,0:T(8,128)(2,1)}, f32[512,768]{1,0:T(8,128)}, f32[3,48,384]{2,1,0:T(8,128)}, f32[48,384]{1,0:T(8,128)}, f32[2,24]{1,0:T(2,128)...) custom-call(f32[512,768]{1,0:T(8,128)} %get-tuple-element.59.base_re, ...), custom_call_target="tpu_custom_call" | custom-call | tf_op jit(solution)/shard_map/pallas_call | solution.py:595
  303.2 1.3 slice_bitcast_fusion
  (1 shorter events, 0.0 us)
